TPU v7x, 256 devices: a whole 4x4x8 slice. The times are simulated.
256 devices in a mesh: energy: 32 (over x, y, core), space: 8 (over z).
Axes of the slice: x: 4, y: 4, z: 8, core: 2. Of those that a mesh axis runs over, the one named last changes fastest.
Arguments:
- onsite: float32 [8, 2, 128, 128], P('space'), may hold values from -0.25 to 0.25
- hopping: float32 [8, 2, 128, 128], P('space'), may hold values from -0.25 to 0.25
- sigma_old: float32 [32, 8, 2, 128, 128], P('energy', 'space'), may hold values from -0.0390625 to 0.0390625
- screened: float32 [32, 8, 2, 3, 2, 128, 128], P('energy', 'space'), may hold values from -1 to 1
Outputs:
- green_retarded: float32 [32, 8, 3, 2, 128, 128], P('energy', 'space')
- self_energy: float32 [32, 8, 2, 3, 2, 128, 128], P('energy', 'space')
All inputs are finite; a program needn't handle non-finite values.
Results may differ from a plain program's by a relative error of at most 0.0003.
Values sent between devices are 32-bit elements; how exact they have to be, the bound alone decides.
A program may use at most 128 MiB of HBM per device.

v0:
```python
import math

import jax
import jax.numpy as jnp
from jax import lax
from jax.sharding import PartitionSpec as P

BROADEN = 0.45
THERMAL = 0.1
PRECISE = lax.Precision.HIGHEST


def passed_along(block, axis, distance):
    devices = range(lax.axis_size(axis))
    route = [(i - distance, i) for i in devices if i - distance in devices]
    return lax.ppermute(block, axis, route)


def matmul_high(first, second):
    return jnp.matmul(first, second, precision=PRECISE)


def complex_product(first, second):
    real_part = matmul_high(first[0], second[0]) - matmul_high(first[1], second[1])
    imag_part = matmul_high(first[0], second[1]) + matmul_high(first[1], second[0])
    return jnp.stack([real_part, imag_part])


def dagger(blocks):
    return jnp.stack([jnp.swapaxes(blocks[0], -1, -2), -jnp.swapaxes(blocks[1], -1, -2)])


def invert(blocks):
    size_order = blocks.shape[-1]
    normal_complex = complex_product(dagger(blocks), blocks)
    upper_normal = jnp.concatenate([normal_complex[0], -normal_complex[1]], axis=-1)
    lower_normal = jnp.concatenate([normal_complex[1], normal_complex[0]], axis=-1)
    normal = jnp.concatenate([upper_normal, lower_normal], axis=-2)
    factor = jnp.linalg.cholesky(normal)
    right_side = jnp.concatenate(
        [jnp.swapaxes(blocks[0], -1, -2), -jnp.swapaxes(blocks[1], -1, -2)], axis=-2
    )
    middle = lax.linalg.triangular_solve(factor, right_side, left_side=True, lower=True)
    solved = lax.linalg.triangular_solve(
        factor, middle, left_side=True, lower=True, transpose_a=True
    )
    return jnp.stack([solved[..., :size_order, :], solved[..., size_order:, :]])


def spectrum_forward(cosines, sines, values):
    energies_all = values.shape[0]
    real_part = values[:, :, :, 0].reshape(energies_all, -1)
    imag_part = values[:, :, :, 1].reshape(energies_all, -1)
    return (
        matmul_high(cosines, real_part) + matmul_high(sines, imag_part),
        matmul_high(cosines, imag_part) - matmul_high(sines, real_part),
    )


def paired_inverse(system_pair, outer_pair, carried, inner_pair):
    return invert(system_pair - complex_product(outer_pair, complex_product(carried, inner_pair)))


def local(onsite, hopping, sigma_old, screened):
    local_count = sigma_old.shape[0]
    size_order = sigma_old.shape[-1]
    groups = lax.axis_size("energy")
    energies_all = local_count * groups
    segments = lax.axis_size("space")
    position = lax.axis_index("space")
    is_first = position == 0
    indices = (lax.axis_index("energy") * local_count + jnp.arange(local_count)).astype(jnp.float32)
    energy = -1.5 + 3.0 * (indices + 0.5) / energies_all
    identity = jnp.eye(size_order, dtype=jnp.float32)
    hamiltonian = 0.5 * (onsite[0] + dagger(onsite[0]))
    coupling = hopping[0]
    local_sigma = jnp.moveaxis(sigma_old[:, 0], 1, 0)
    system = jnp.stack(
        [
            energy[:, None, None] * identity - hamiltonian[0] - local_sigma[0],
            BROADEN * identity - hamiltonian[1] - local_sigma[1],
        ]
    )
    magnitude = energy * energy + BROADEN * BROADEN
    contact_green = jnp.stack(
        [
            (energy / magnitude)[:, None, None] * identity,
            (-BROADEN / magnitude)[:, None, None] * identity,
        ]
    )
    next_coupling = passed_along(coupling, "space", -1)
    system_pair = jnp.stack([system, system], axis=1)
    outer_pair = jnp.stack([dagger(coupling), next_coupling], axis=1)[:, :, None]
    inner_pair = jnp.stack([coupling, dagger(next_coupling)], axis=1)[:, :, None]

    def sweep(iteration, received):
        fresh = paired_inverse(system_pair, outer_pair, received, inner_pair)
        got_left = passed_along(fresh[:, 0], "space", 1)
        got_left = jnp.where(is_first, contact_green, got_left)
        got_right = passed_along(fresh[:, 1], "space", -1)
        return jnp.stack([got_left, got_right], axis=1)

    start_left = jnp.where(is_first, contact_green, jnp.zeros_like(contact_green))
    start_pair = jnp.stack([start_left, jnp.zeros_like(contact_green)], axis=1)
    final_pair = lax.fori_loop(0, segments - 1, sweep, start_pair)
    previous = final_pair[:, 0]
    following = final_pair[:, 1]
    self_left = complex_product(dagger(coupling), complex_product(previous, coupling))
    self_right = complex_product(next_coupling, complex_product(following, dagger(next_coupling)))
    diagonal = invert(system - self_left - self_right)
    upper_block = complex_product(previous, complex_product(coupling, diagonal))
    lower_block = complex_product(diagonal, complex_product(dagger(coupling), previous))
    stacked = jnp.stack([diagonal, upper_block, lower_block], axis=2)
    green_out = jnp.transpose(stacked, (1, 2, 0, 3, 4))[:, None]
    spectral = jnp.stack(
        [
            diagonal - dagger(diagonal),
            upper_block - dagger(lower_block),
            lower_block - dagger(upper_block),
        ],
        axis=2,
    )
    kernels = screened.reshape(local_count, 2, 3, 2, size_order * size_order)
    occupation = 1.0 / (1.0 + jnp.exp(energy / THERMAL))
    occupied = occupation[None, :, None, None, None]
    both_kinds = jnp.stack([-occupied * spectral, (1.0 - occupied) * spectral])
    outgoing = jnp.transpose(both_kinds, (2, 0, 3, 1, 4, 5)).reshape(
        local_count, 2, 3, 2, size_order * size_order
    )
    gathered, spectra = (
        lax.all_to_all(outgoing, "energy", split_axis=4, concat_axis=0, tiled=True),
        lax.all_to_all(kernels, "energy", split_axis=4, concat_axis=0, tiled=True),
    )
    padded_length = 2 * energies_all
    frequency = jnp.arange(padded_length, dtype=jnp.int32)[:, None]
    position_grid = jnp.arange(energies_all, dtype=jnp.int32)[None, :]
    phases = (frequency * position_grid % padded_length).astype(jnp.float32) * (
        2.0 * math.pi / padded_length
    )
    cosines = jnp.cos(phases)
    sines = jnp.sin(phases)
    green_real, green_imag = spectrum_forward(cosines, sines, gathered)
    kernel_real, kernel_imag = spectrum_forward(cosines, sines, spectra)
    product_real = green_real * kernel_real - green_imag * kernel_imag
    product_imag = green_real * kernel_imag + green_imag * kernel_real
    back_cosines = jnp.transpose(cosines) / padded_length
    back_sines = jnp.transpose(sines) / padded_length
    conv_real = matmul_high(back_cosines, product_real) - matmul_high(back_sines, product_imag)
    conv_imag = matmul_high(back_cosines, product_imag) + matmul_high(back_sines, product_real)
    slice_width = gathered.shape[-1]
    conv_real = conv_real.reshape(energies_all, 2, 3, slice_width)
    conv_imag = conv_imag.reshape(energies_all, 2, 3, slice_width)
    sigma_elements = jnp.stack([-conv_imag, conv_real], axis=3)
    sigma_local = lax.all_to_all(sigma_elements, "energy", split_axis=0, concat_axis=4, tiled=True)
    sigma_out = sigma_local.reshape(local_count, 1, 2, 3, 2, size_order, size_order)
    return (green_out, sigma_out)


def solution(mesh):
    placed = (
        P("space", None, None, None),
        P("space", None, None, None),
        P("energy", "space", None, None, None),
        P("energy", "space", None, None, None, None, None),
    )
    return jax.shard_map(
        local,
        mesh=mesh,
        in_specs=placed,
        out_specs=(
            P("energy", "space", None, None, None, None),
            P("energy", "space", None, None, None, None, None),
        ),
        check_vma=False,
    )
```

profile of v0, /device:TPU:1, one launch (start us, length us, event | category | flops | bytes accessed | tf_op | source)
XLA Modules:
  0.0 1384.2 jit_solution(7943360227580603645)
XLA Ops:
  3.1 24.3 %copy.351 = f32[1,1,2,3,2,128,128]{3,4,2,6,5,1,0:T(2,128)} copy(f32[1,1,2,3,2,128,128]{6,5,4,3,2,1,0:T(8,128)} %param.9) | data formatting | bytes 1572864 | tf_op args[3]
  27.5 50.3 %reshape.1289 = f32[32,1,6144]{2,1,0:T(1,128)} reshape(f32[16384,1,2,2,3]{4,3,2,1,0:T(2,128)} %bitcast.664) | data formatting | bytes 1572864
  87.5 894.0 %while.14 = (s32[]{:T(128)}, f32[2,2,1,128,128]{4,3,0,2,1:T(8,128)S(1)}, pred[]{:T(512)}, f32[2,2,1,128,128]{4,3,1,2,0:T(8,128)S(1)}, f32[2,2,1,128,128]{4,3,1,2...) while((s32[]{:T(128)}, ...), condition=%wide.region_5.6_spmd, body=%wide.region_0.5_spmd.sunk | while | flops 1009058304 | bytes 19206544 | solution.py:105
  92.7 23.5 %custom-call.47 = f32[2,1,128,128]{3,2,1,0:T(8,128)S(1)} custom-call(f32[2,1,128,128]{3,2,1,0:T(8,128)S(1)} %cholesky.395), custom_call_target="Cholesky" | custom-call | tf_op jit(solution)/shard_map/while/body/eval_jaxpr/jit(cholesky)/cholesky | solution.py:39
  136.6 23.5 %custom-call.49 = f32[2,1,128,128]{3,2,1,0:T(8,128)S(1)} custom-call(f32[2,1,128,128]{3,2,1,0:T(8,128)S(1)} %fusion.435), custom_call_target="Cholesky" | custom-call | tf_op jit(solution)/shard_map/while/body/eval_jaxpr/jit(cholesky)/cholesky | solution.py:39
  164.5 39.3 %custom-call.51 = f32[2,1,2,128,128]{3,4,2,1,0:T(8,128)S(1)} custom-call(f32[2,1,2,128,128]{4,3,2,1,0:T(8,128)S(1)} %bitcast.691), custom_call_target="InvertDiagBlocksLowerTriangular" | custom-call | tf_op jit(solution)/shard_map/while/body/eval_jaxpr/triangular_solve | solution.py:44
  221.7 23.5 %custom-call.47 = f32[2,1,128,128]{3,2,1,0:T(8,128)S(1)} custom-call(f32[2,1,128,128]{3,2,1,0:T(8,128)S(1)} %cholesky.395), custom_call_target="Cholesky" | custom-call | tf_op jit(solution)/shard_map/while/body/eval_jaxpr/jit(cholesky)/cholesky | solution.py:39
  265.5 23.5 %custom-call.49 = f32[2,1,128,128]{3,2,1,0:T(8,128)S(1)} custom-call(f32[2,1,128,128]{3,2,1,0:T(8,128)S(1)} %fusion.435), custom_call_target="Cholesky" | custom-call | tf_op jit(solution)/shard_map/while/body/eval_jaxpr/jit(cholesky)/cholesky | solution.py:39
  293.4 39.3 %custom-call.51 = f32[2,1,2,128,128]{3,4,2,1,0:T(8,128)S(1)} custom-call(f32[2,1,2,128,128]{4,3,2,1,0:T(8,128)S(1)} %bitcast.691), custom_call_target="InvertDiagBlocksLowerTriangular" | custom-call | tf_op jit(solution)/shard_map/while/body/eval_jaxpr/triangular_solve | solution.py:44
  350.4 23.5 %custom-call.47 = f32[2,1,128,128]{3,2,1,0:T(8,128)S(1)} custom-call(f32[2,1,128,128]{3,2,1,0:T(8,128)S(1)} %cholesky.395), custom_call_target="Cholesky" | custom-call | tf_op jit(solution)/shard_map/while/body/eval_jaxpr/jit(cholesky)/cholesky | solution.py:39
  394.2 23.5 %custom-call.49 = f32[2,1,128,128]{3,2,1,0:T(8,128)S(1)} custom-call(f32[2,1,128,128]{3,2,1,0:T(8,128)S(1)} %fusion.435), custom_call_target="Cholesky" | custom-call | tf_op jit(solution)/shard_map/while/body/eval_jaxpr/jit(cholesky)/cholesky | solution.py:39
  422.1 39.3 %custom-call.51 = f32[2,1,2,128,128]{3,4,2,1,0:T(8,128)S(1)} custom-call(f32[2,1,2,128,128]{4,3,2,1,0:T(8,128)S(1)} %bitcast.691), custom_call_target="InvertDiagBlocksLowerTriangular" | custom-call | tf_op jit(solution)/shard_map/while/body/eval_jaxpr/triangular_solve | solution.py:44
  478.3 23.5 %custom-call.47 = f32[2,1,128,128]{3,2,1,0:T(8,128)S(1)} custom-call(f32[2,1,128,128]{3,2,1,0:T(8,128)S(1)} %cholesky.395), custom_call_target="Cholesky" | custom-call | tf_op jit(solution)/shard_map/while/body/eval_jaxpr/jit(cholesky)/cholesky | solution.py:39
  522.2 23.5 %custom-call.49 = f32[2,1,128,128]{3,2,1,0:T(8,128)S(1)} custom-call(f32[2,1,128,128]{3,2,1,0:T(8,128)S(1)} %fusion.435), custom_call_target="Cholesky" | custom-call | tf_op jit(solution)/shard_map/while/body/eval_jaxpr/jit(cholesky)/cholesky | solution.py:39
  550.1 39.3 %custom-call.51 = f32[2,1,2,128,128]{3,4,2,1,0:T(8,128)S(1)} custom-call(f32[2,1,2,128,128]{4,3,2,1,0:T(8,128)S(1)} %bitcast.691), custom_call_target="InvertDiagBlocksLowerTriangular" | custom-call | tf_op jit(solution)/shard_map/while/body/eval_jaxpr/triangular_solve | solution.py:44
  677.3 39.3 %custom-call.51 = f32[2,1,2,128,128]{3,4,2,1,0:T(8,128)S(1)} custom-call(f32[2,1,2,128,128]{4,3,2,1,0:T(8,128)S(1)} %bitcast.691), custom_call_target="InvertDiagBlocksLowerTriangular" | custom-call | tf_op jit(solution)/shard_map/while/body/eval_jaxpr/triangular_solve | solution.py:44
  804.6 39.3 %custom-call.51 = f32[2,1,2,128,128]{3,4,2,1,0:T(8,128)S(1)} custom-call(f32[2,1,2,128,128]{4,3,2,1,0:T(8,128)S(1)} %bitcast.691), custom_call_target="InvertDiagBlocksLowerTriangular" | custom-call | tf_op jit(solution)/shard_map/while/body/eval_jaxpr/triangular_solve | solution.py:44
  931.1 39.3 %custom-call.51 = f32[2,1,2,128,128]{3,4,2,1,0:T(8,128)S(1)} custom-call(f32[2,1,2,128,128]{4,3,2,1,0:T(8,128)S(1)} %bitcast.691), custom_call_target="InvertDiagBlocksLowerTriangular" | custom-call | tf_op jit(solution)/shard_map/while/body/eval_jaxpr/triangular_solve | solution.py:44
  1055.1 30.3 %copy.347 = f32[1,2,3,2,16384]{2,3,1,0,4:T(2,128)} copy(f32[1,2,3,2,16384]{4,0,3,2,1:T(1,128)S(1)} %bitcast.676) | data formatting | bytes 1572864 | tf_op jit(solution)/shard_map/reshape | solution.py:127
  1085.4 50.3 %reshape.1287 = f32[32,1,6144]{2,1,0:T(1,128)} reshape(f32[16384,1,2,2,3]{4,3,2,1,0:T(2,128)} %bitcast.661) | data formatting | bytes 1572864
  1156.8 64.8 %reshape.1290 = f32[16384,1,2,2,3]{4,3,2,1,0:T(2,128)} reshape(f32[32,6144]{1,0:T(8,128)S(1)} %reduce.36) | data formatting | bytes 1572864
  1221.6 26.7 %copy.380 = f32[1,2,3,2,32,512]{5,4,3,2,1,0:T(8,128)S(1)} copy(f32[1,2,3,2,32,512]{2,3,1,5,4,0:T(2,128)} %bitcast.662) | data formatting | bytes 1572864 | tf_op jit(solution)/shard_map/all_to_all | solution.py:132
  1255.7 65.0 %reshape.1288 = f32[16384,1,2,2,3]{4,3,2,1,0:T(2,128)} reshape(f32[32,6144]{1,0:T(8,128)S(1)} %reduce.37) | data formatting | bytes 1572864
  1320.7 26.9 %copy.379 = f32[1,2,3,2,32,512]{5,4,3,2,1,0:T(8,128)S(1)} copy(f32[1,2,3,2,32,512]{2,3,1,5,4,0:T(2,128)} %bitcast.663) | data formatting | bytes 1572864 | tf_op jit(solution)/shard_map/all_to_all | solution.py:131
  (551 shorter events, 607.9 us)
Async XLA Ops:
  1.6 84.8 %copy-start = (f32[1,2,128,128]{3,2,1,0:T(8,128)S(1)}, f32[1,2,128,128]{3,2,1,0:T(8,128)}, u32[]{:S(2)}) copy-start(f32[1,2,128,128]{3,2,1,0:T(8,128)} %param.7) | copy-start | bytes 393220
  1.6 84.9 %copy-start.9 = (f32[1,2,128,128]{3,2,1,0:T(8,128)S(1)}, f32[1,2,128,128]{3,2,1,0:T(8,128)}, u32[]{:S(2)}) copy-start(f32[1,2,128,128]{3,2,1,0:T(8,128)} %param.6) | copy-start | bytes 393220
  1.7 85.2 %copy-start.11 = (f32[1,1,2,128,128]{4,3,2,1,0:T(8,128)S(1)}, f32[1,1,2,128,128]{4,3,2,1,0:T(8,128)}, u32[]{:S(2)}) copy-start(f32[1,1,2,128,128]{4,3,2,1,0:T(8,128)} %param.8) | copy-start | bytes 393220
  1.7 85.6 %collective-permute-start.2 = (f32[2,128,128]{1,2,0:T(8,128)S(1)}, f32[2,128,128]{1,2,0:T(8,128)S(1)}, u32[]{:S(2)}, u32[]{:S(2)}) collective-permute-start(f32[2,128,128]{1,2,0:T(8,128)S(1)} %bitcast.690), channel_id=1, source_target_pairs={{1,0},{2,1},{3,2},{4,3},{5,4},{6,5},{7,6},{9,8},{10,9},{11,10},{12... | collective-permute-start | bytes 393224 | tf_op jit(solution)/shard_map/ppermute | solution.py:16
  77.7 1057.9 %all-to-all-start.1 = ((f32[32,1,6144]{2,1,0:T(1,128)}), f32[32,1,6144]{2,1,0:T(1,128)}, u32[]{:S(2)}, u32[]{:S(2)}) async-start(f32[32,1,6144]{2,1,0:T(1,128)} %reshape.1289), calls=%async_computation.1 | async-start | bytes 1572864 | tf_op jit(solution)/shard_map/all_to_all | solution.py:132
  205.9 6.8 collective-permute-start.1
  210.1 6.7 collective-permute-start
  334.8 5.5 collective-permute-start.1
  338.4 7.2 collective-permute-start
  463.5 6.2 collective-permute-start.1
  467.8 5.7 collective-permute-start
  591.4 5.5 collective-permute-start.1
  595.0 5.8 collective-permute-start
  718.7 5.6 collective-permute-start.1
  722.4 5.7 collective-permute-start
  846.0 4.7 collective-permute-start.1
  848.8 5.7 collective-permute-start
  972.4 5.1 collective-permute-start.1
  975.6 5.7 collective-permute-start
  1135.7 117.5 %all-to-all-start = ((f32[32,1,6144]{2,1,0:T(1,128)}), f32[32,1,6144]{2,1,0:T(1,128)S(1)}, u32[]{:S(2)}, u32[]{:S(2)}) async-start(f32[32,1,6144]{2,1,0:T(1,128)} %reshape.1287), calls=%async_computation | async-start | bytes 1572864 | tf_op jit(solution)/shard_map/all_to_all | solution.py:131
  1320.7 47.9 %copy-start.4 = (f32[128,128]{0,1:T(8,128)S(1)}, f32[128,128]{0,1:T(8,128)}, u32[]{:S(2)}) copy-start(f32[128,128]{0,1:T(8,128)} %copy-done.3) | copy-start | bytes 196612
  1320.7 48.0 %copy-start.6 = (f32[128,128]{0,1:T(8,128)S(1)}, f32[128,128]{0,1:T(8,128)}, u32[]{:S(2)}) copy-start(f32[128,128]{0,1:T(8,128)} %copy-done.5) | copy-start | bytes 196612
  1320.7 48.0 %copy-start.8 = (f32[1,1,128,128]{2,3,0,1:T(8,128)S(1)}, f32[1,1,128,128]{2,3,0,1:T(8,128)}, u32[]{:S(2)}) copy-start(f32[1,1,128,128]{2,3,0,1:T(8,128)} %copy-done.7) | copy-start | bytes 196612
  1361.1 21.6 %all-to-all-start.2 = ((f32[32,2,3,2,512]{4,3,2,1,0:T(2,128)}), f32[32,2,3,2,512]{4,3,2,1,0:T(2,128)S(1)}, u32[]{:S(2)}, u32[]{:S(2)}) async-start(f32[32,2,3,2,512]{4,3,2,1,0:T(2,128)} %copy.355), calls=%async_computation.2 | async-start | bytes 1572864 | tf_op jit(solution)/shard_map/all_to_all | solution.py:154
  (6 other events, 103.0 us)
where the time goes:
time: 1390 us; the launch traced here: 1380 us
  other arithmetic  808 us (58%)
  local copies, waits for them, and re-layouts  384 us (28%)
  matrix products  70.8 us (5%)
  starting transfers between devices  68.7 us (5%)
  waiting for transfers between devices  46.4 us (3%)
    another operation x70, other arithmetic, invert(): factor = jnp.linalg.cholesky(normal)  503 us
    another operation x31, other arithmetic, invert(): lax.linalg.triangular_solve(factor, middle, left_side=True, lower=True, t...  296 us
    unnamed x33, local copies, waits for them, and re-layouts  257 us
    dot_general x132, matrix products, matmul_high(): return jnp.matmul(first, second, precision=PRECISE)  50.5 us
    ppermute x15, starting transfers between devices, passed_along(): return lax.ppermute(block, axis, route)  35.7 us
    ppermute x15, waiting for transfers between devices, passed_along(): return lax.ppermute(block, axis, route)  33.3 us
    another operation x48, local copies, waits for them, and re-layouts  31.5 us
    reshape x1, local copies, waits for them, and re-layouts, local(): jnp.transpose(both_kinds, (2, 0, 3, 1, 4, 5))  30.3 us
  transfers between devices with their start and end apart: 18, of which 15 were waited for; matrix products, arithmetic and copies ran while one was open for 83% of the time, Pallas kernels for 0%

commit v1 on v0

v1 whole, which is shorter than its diff:
```python
import jax
import jax.numpy as jnp
from jax import lax
from jax.experimental import pallas as pl
from jax.experimental.pallas import tpu as pltpu
from jax.sharding import PartitionSpec as P

BROADEN = 0.45
THERMAL = 0.1
B = 128
NE = 32
NC = 8
PANEL = 16
MESH = pl.DeviceIdType.MESH
F32 = jnp.float32


def split(x):
    high = x.astype(jnp.bfloat16)
    return high, (x - high.astype(F32)).astype(jnp.bfloat16)


def dot(a, b):
    return lax.dot_general(a, b, (((1,), (0,)), ((), ())), preferred_element_type=F32)


def product(xr, xi, yr, yi):
    left = jnp.concatenate([xr, xi], axis=1)
    right = jnp.concatenate(
        [jnp.concatenate([yr, yi], axis=1), jnp.concatenate([-yi, yr], axis=1)], axis=0
    )
    lh, ll = split(left)
    rh, rl = split(right)
    out = dot(lh, rh) + (dot(lh, rl) + dot(ll, rh))
    return out[:, :B], out[:, B:]


def mm(x, y):
    return product(x[0], x[1], y[0], y[1])


def put(ref, pair):
    ref[0] = pair[0]
    ref[1] = pair[1]


def put_dagger(ref, x):
    ref[0] = x[0].T
    ref[1] = -x[1].T


def tile_inverse(tr, ti, off, lane, sub):
    shape = tr.shape
    cols = [
        (
            jnp.broadcast_to(tr[:, off + j : off + j + 1], shape),
            jnp.broadcast_to(ti[:, off + j : off + j + 1], shape),
        )
        for j in range(8)
    ]
    for k in range(8):
        cr, ci = cols[k]
        pr = jnp.broadcast_to(cr[k : k + 1], shape)
        pi = jnp.broadcast_to(ci[k : k + 1], shape)
        inv = 1.0 / (pr * pr + pi * pi)
        qr = pr * inv
        qi = -(pi * inv)
        own = sub == k
        mr = jnp.where(own, -qr, cr * qr - ci * qi)
        mi = jnp.where(own, -qi, cr * qi + ci * qr)

        def step(xr, xi):
            br = jnp.broadcast_to(xr[k : k + 1], shape)
            bi = jnp.broadcast_to(xi[k : k + 1], shape)
            return (
                jnp.where(own, 0.0, xr) - (mr * br - mi * bi),
                jnp.where(own, 0.0, xi) - (mr * bi + mi * br),
            )

        for j in range(k + 1, 8):
            cols[j] = step(*cols[j])
        here = lane == off + k
        tr, ti = step(
            jnp.where(here, jnp.where(own, 1.0, 0.0), tr), jnp.where(here, 0.0, ti)
        )
    return tr, ti


def panel_inverse(pr, pi):
    shape = (8, B)
    lane = lax.broadcasted_iota(jnp.int32, shape, 1)
    sub = lax.broadcasted_iota(jnp.int32, shape, 0)
    tiles = [(pr[8 * t : 8 * t + 8], pi[8 * t : 8 * t + 8]) for t in range(PANEL // 8)]
    for t in range(len(tiles)):
        off = 8 * t
        tiles[t] = tile_inverse(*tiles[t], off, lane, sub)
        tr, ti = tiles[t]
        active = (lane >= off) & (lane < off + 8)
        for u in range(len(tiles)):
            if u == t:
                continue
            xr, xi = tiles[u]
            sr, si = jnp.zeros(shape, F32), jnp.zeros(shape, F32)
            for j in range(8):
                cr = jnp.broadcast_to(xr[:, off + j : off + j + 1], shape)
                ci = jnp.broadcast_to(xi[:, off + j : off + j + 1], shape)
                rr = jnp.broadcast_to(tr[j : j + 1], shape)
                ri = jnp.broadcast_to(ti[j : j + 1], shape)
                sr = sr + (cr * rr - ci * ri)
                si = si + (cr * ri + ci * rr)
            tiles[u] = (jnp.where(active, 0.0, xr) - sr, jnp.where(active, 0.0, xi) - si)
    return jnp.concatenate([x[0] for x in tiles]), jnp.concatenate([x[1] for x in tiles])


def invert(x):
    rest, back = B - PANEL, B - PANEL
    lane = lax.broadcasted_iota(jnp.int32, (rest, B), 1)

    def body(_, panel):
        xr, xi = x[0, PANEL:, :], x[1, PANEL:, :]
        columns = jnp.concatenate([xr[:, :PANEL], xi[:, :PANEL]], axis=1)
        ch, cl = split(columns)
        x[0, :rest, :] = pltpu.roll(jnp.where(lane < PANEL, 0.0, xr), back, 1)
        x[1, :rest, :] = pltpu.roll(jnp.where(lane < PANEL, 0.0, xi), back, 1)
        rr, ri = panel_inverse(*panel)
        rr, ri = pltpu.roll(rr, back, 1), pltpu.roll(ri, back, 1)
        rows = jnp.concatenate(
            [jnp.concatenate([rr, ri], axis=1), jnp.concatenate([-ri, rr], axis=1)], axis=0
        )
        rh, rl = split(rows)
        update = dot(
            jnp.concatenate([ch, ch, cl], axis=1), jnp.concatenate([rh, rl, rh], axis=0)
        )
        nr = x[0, :rest, :] - update[:, :B]
        ni = x[1, :rest, :] - update[:, B:]
        x[0, :rest, :] = nr
        x[1, :rest, :] = ni
        x[0, rest:, :] = rr
        x[1, rest:, :] = ri
        return nr[:PANEL], ni[:PANEL]

    lax.fori_loop(0, B // PANEL, body, (x[0, :PANEL, :], x[1, :PANEL, :]))


def kernel(
    onsite, hopping, sigma, screened, green, out,
    ahead, arrived, middle, outer, x, m, k1, k1h, k2, k2h, t, v, p, q2,
    spectral, wbuf, dbuf, scaled, factor, sbuf,
    s_hop, s_chain, s_mid, s_out, s_w, s_d, s_relay, s_sig,
    r_hop, r_chain, r_mid, r_out, r_w, r_d, r_relay, r_sig,
):
    e = lax.axis_index("energy")
    j = lax.axis_index("space")
    chip, core = e // 2, e % 2
    cx, cy = chip // 4, chip % 4
    left = j < NC // 2
    is_mid = (j == NC // 2 - 1) | (j == NC // 2)
    row = pl.multiple_of(chip * 8, 8)

    def relative(i):
        return ((cx + i // 4) % 4) * 4 + (cy + i % 4) % 4

    barrier = pltpu.get_barrier_semaphore()

    def greet(i, c):
        pl.semaphore_signal(
            barrier, inc=1, device_id={"energy": (e + i) % NE}, device_id_type=MESH
        )
        return c

    for step in (1, NC - 1):
        pl.semaphore_signal(
            barrier, inc=1, device_id={"space": (j + step) % NC}, device_id_type=MESH
        )
    lax.fori_loop(1, NE, greet, 0)

    def energy_of(n, shape):
        return -1.5 + 3.0 * (jnp.full(shape, n, jnp.int32).astype(F32) + 0.5) / NE

    eye = lax.broadcasted_iota(jnp.int32, (B, B), 0) == lax.broadcasted_iota(
        jnp.int32, (B, B), 1
    )
    en = energy_of(e, (B, B))
    on_r, on_i = onsite[0, 0], onsite[0, 1]
    m[0] = jnp.where(eye, en, 0.0) - 0.5 * (on_r + on_r.T) - sigma[0, 0, 0]
    m[1] = jnp.where(eye, BROADEN, 0.0) - 0.5 * (on_i - on_i.T) - sigma[0, 0, 1]
    hop = hopping.at[0]

    @pl.when(left)
    def _():
        put(k1, hop)
        put_dagger(k1h, hop)

    @pl.when(jnp.logical_not(left))
    def _():
        put(k2h, hop)
        put_dagger(k2, hop)

    @pl.when(j == 0)
    def _():
        size = en * en + BROADEN * BROADEN
        arrived[0] = jnp.where(eye, en / size, 0.0)
        arrived[1] = jnp.where(eye, -BROADEN / size, 0.0)

    @pl.when(j == NC - 1)
    def _():
        for ref in (arrived, k1, k1h):
            ref[...] = jnp.zeros_like(ref)

    pl.semaphore_wait(barrier, NE - 1 + 2)

    def to_space(src, dst, s, r, where):
        return pltpu.make_async_remote_copy(
            src_ref=src, dst_ref=dst, send_sem=s, recv_sem=r,
            device_id={"space": where}, device_id_type=MESH,
        )

    def to_energy(src, dst, s, r, where):
        return pltpu.make_async_remote_copy(
            src_ref=src, dst_ref=dst, send_sem=s, recv_sem=r,
            device_id={"energy": where}, device_id_type=MESH,
        )

    down = jnp.maximum(j - 1, 0)
    up = jnp.minimum(j + 1, NC - 1)
    inner = jnp.where(left, up, down)
    outward = jnp.where(left, down, up)
    hop_copy = to_space(hop, ahead, s_hop, r_hop, down)

    @pl.when(j > 0)
    def _():
        hop_copy.start()

    def send_w(i, c):
        other = relative(i // 2)
        kind = (core + i % 2) % 2
        to_energy(
            screened.at[0, 0, kind, :, :, pl.ds(pl.multiple_of(other * 8, 8), 8), :],
            wbuf.at[e], s_w, r_w, other * 2 + kind,
        ).start()
        return c

    lax.fori_loop(1, NE, send_w, 0)
    wbuf[e] = screened[0, 0, core, :, :, pl.ds(row, 8), :]

    @pl.when(jnp.logical_not(left) & (j < NC - 1))
    def _():
        hop_copy.wait_recv()
        put(k1h, ahead)
        put_dagger(k1, ahead)

    def occupations(n, c):
        f = 1.0 / (1.0 + jnp.exp(energy_of(n, (8, B)) / THERMAL))
        factor[n] = jnp.where(jnp.full((8, B), core, jnp.int32) == 0, -f, 1.0 - f)
        return c

    chain = to_space(x, arrived, s_chain, r_chain, inner)
    meet = to_space(x, middle, s_mid, r_mid, inner)

    @pl.when((j > 0) & (j < NC - 1))
    def _():
        chain.wait_recv()

    put(t, mm(k1h, arrived))
    sr, si = mm(t, k1)
    m[0] = m[0] - sr
    m[1] = m[1] - si
    x[...] = m[...]
    invert(x)

    @pl.when(jnp.logical_not(is_mid))
    def _():
        chain.start()

    @pl.when(is_mid)
    def _():
        meet.start()

    lax.fori_loop(0, NE, occupations, 0)
    for n in range(8):
        scaled[n] = jnp.zeros_like(scaled[n])

    @pl.when(left)
    def _():
        hop_copy.wait_recv()
        put(k2, ahead)
        put_dagger(k2h, ahead)
        put(v, mm(arrived, k1))

    g = green.at[0, 0, 0]
    onward = to_space(g, outer, s_out, r_out, outward)

    @pl.when(is_mid)
    def _():
        meet.wait_recv()
        ar, ai = mm(k2, middle)
        sr, si = product(ar, ai, k2h[0], k2h[1])
        g[0] = m[0] - sr
        g[1] = m[1] - si
        invert(g)
        onward.start()

        @pl.when(j == NC // 2)
        def _():
            put(t, (ar, ai))
            put(v, mm(middle, k2h))

    @pl.when(jnp.logical_not(is_mid))
    def _():
        put(p, mm(x, k2))
        put(q2, mm(k2h, x))
        onward.wait_recv()
        put(m, mm(p, outer))
        ar, ai = mm(m, q2)
        g[0] = x[0] + ar
        g[1] = x[1] + ai

        @pl.when((j > 0) & (j < NC - 1))
        def _():
            onward.start()

    @pl.when(j <= NC // 2)
    def _():
        put(green.at[0, 0, 1], mm(v, g))
        put(green.at[0, 0, 2], mm(g, t))

    @pl.when(j > NC // 2)
    def _():
        put(green.at[0, 0, 1], mm(outer, q2))
        put(green.at[0, 0, 2], (m[0], m[1]))

    u, w = green.at[0, 0, 1], green.at[0, 0, 2]
    spectral[0, 0] = g[0] - g[0].T
    spectral[0, 1] = g[1] + g[1].T
    dr = u[0] - w[0].T
    di = u[1] + w[1].T
    spectral[1, 0] = dr
    spectral[1, 1] = di
    spectral[2, 0] = -dr.T
    spectral[2, 1] = di.T

    def send_d(i, c):
        other = relative(i)
        to_energy(
            spectral.at[:, :, pl.ds(pl.multiple_of(other * 8, 8), 8), :],
            dbuf.at[core, chip], s_d, r_d, other * 2 + core,
        ).start()
        return c

    lax.fori_loop(1, NE // 2, send_d, 0)
    dbuf[core, chip] = spectral[:, :, pl.ds(row, 8), :]
    some = dbuf.at[0, pl.ds(0, NE // 2 - 1)]
    to_energy(some, some, s_d, r_d, e).wait_recv()
    relay = to_energy(dbuf.at[core], dbuf.at[core], s_relay, r_relay, chip * 2 + 1 - core)
    relay.start()
    many = wbuf.at[pl.ds(0, NE - 1)]
    to_energy(many, many, s_w, r_w, e).wait_recv()
    relay.wait_recv()

    def scale(n, c):
        scaled[8 + n] = dbuf[n % 2, n // 2] * factor[n]
        return c

    lax.fori_loop(0, NE, scale, 0)

    def convolve(turn, c):
        start = ((cx + turn) % 4) * 8
        for b in range(3):
            zero = jnp.zeros((8, B), F32)

            def add(k, acc):
                wr, wi = wbuf[k, b, 0], wbuf[k, b, 1]
                new = []
                for i in range(8):
                    lr = scaled[8 + start + i - k, b, 0]
                    li = scaled[8 + start + i - k, b, 1]
                    ar, ai = acc[i]
                    new.append((ar + (lr * wr - li * wi), ai + (lr * wi + li * wr)))
                return tuple(new)

            def add8(k, acc):
                for s in range(8):
                    acc = add(k * 8 + s, acc)
                return acc

            acc = lax.fori_loop(0, start // 8 + 1, add8, tuple((zero, zero) for _ in range(8)))
            for i in range(8):
                sbuf[start + i, b, 0] = -acc[i][1]
                sbuf[start + i, b, 1] = acc[i][0]

        def send_s(i, c2):
            n = start + (i + 2 * cy) % 8

            @pl.when(n != e)
            def _():
                to_energy(
                    sbuf.at[n], out.at[0, 0, core, :, :, pl.ds(row, 8), :], s_sig, r_sig, n
                ).start()

            return c2

        lax.fori_loop(0, 8, send_s, 0)
        return c

    lax.fori_loop(0, 4, convolve, 0)
    out[0, 0, core, :, :, pl.ds(row, 8), :] = sbuf[e]

    @pl.when(j > 0)
    def _():
        hop_copy.wait_send()

    @pl.when(jnp.logical_not(is_mid))
    def _():
        chain.wait_send()

    @pl.when(is_mid)
    def _():
        meet.wait_send()

    @pl.when((j > 0) & (j < NC - 1))
    def _():
        onward.wait_send()

    to_energy(many, many, s_w, r_w, e).wait_send()
    to_energy(some, some, s_d, r_d, e).wait_send()
    relay.wait_send()
    to_energy(many, many, s_sig, r_sig, e).wait_send()
    to_energy(many, many, s_sig, r_sig, e).wait_recv()


def local(onsite, hopping, sigma_old, screened):
    vmem = pl.BlockSpec(memory_space=pltpu.VMEM)
    square = pltpu.VMEM((2, B, B), F32)
    return pl.pallas_call(
        kernel,
        out_shape=(
            jax.ShapeDtypeStruct((1, 1, 3, 2, B, B), F32),
            jax.ShapeDtypeStruct((1, 1, 2, 3, 2, B, B), F32),
        ),
        in_specs=[vmem] * 4,
        out_specs=(vmem, vmem),
        scratch_shapes=[square] * 14
        + [
            pltpu.VMEM((3, 2, B, B), F32),
            pltpu.VMEM((NE, 3, 2, 8, B), F32),
            pltpu.VMEM((2, NE // 2, 3, 2, 8, B), F32),
            pltpu.VMEM((NE + 8, 3, 2, 8, B), F32),
            pltpu.VMEM((NE, 8, B), F32),
            pltpu.VMEM((NE, 3, 2, 8, B), F32),
        ]
        + [pltpu.SemaphoreType.DMA] * 16,
        compiler_params=pltpu.CompilerParams(
            collective_id=0, has_side_effects=True, vmem_limit_bytes=48 * 2**20
        ),
        name="transport",
    )(onsite, hopping, sigma_old, screened)


def solution(mesh):
    placed = (
        P("space", None, None, None),
        P("space", None, None, None),
        P("energy", "space", None, None, None),
        P("energy", "space", None, None, None, None, None),
    )
    return jax.shard_map(
        local,
        mesh=mesh,
        in_specs=placed,
        out_specs=(
            P("energy", "space", None, None, None, None),
            P("energy", "space", None, None, None, None, None),
        ),
        check_vma=False,
    )
```

time: 1390 us -> 102 us (0.07)
  other arithmetic: 808 us -> 0 us
  local copies, waits for them, and re-layouts: 384 us -> 5.46 us
  Pallas kernels: 0 us -> 95.6 us
  matrix products: 70.8 us -> 0 us
  starting transfers between devices: 68.7 us -> 0 us
  waiting for transfers between devices: 46.4 us -> 0 us
    another operation x134 -> x0, other arithmetic: 800 us -> none  [the longest x70 503 us: invert(): factor = jnp.linalg.cholesky(normal)]
    unnamed x33 -> x10, local copies, waits for them, and re-layouts: 257 us -> 5.46 us
    pallas_call x0 -> x1, Pallas kernels: none -> 95.6 us  [local(): pl.pallas_call(kernel, out_shape=(jax.ShapeDtypeStruct((1, 1, 3, 2, B, B)...]
    all_to_all x4 -> x0, local copies, waits for them, and re-layouts: 54.3 us -> none  [the longest x2 27.2 us: local(): lax.all_to_all(kernels, 'energy', split_axis=4, concat_axis=0, tiled=True)]
    dot_general x132 -> x0, matrix products: 50.5 us -> none  [matmul_high(): return jnp.matmul(first, second, precision=PRECISE)]
    another operation x85 -> x0, local copies, waits for them, and re-layouts: 36.8 us -> none
    ppermute x15 -> x0, starting transfers between devices: 35.7 us -> none  [passed_along(): return lax.ppermute(block, axis, route)]
    ppermute x15 -> x0, waiting for transfers between devices: 33.3 us -> none  [passed_along(): return lax.ppermute(block, axis, route)]
  transfers between devices with their start and end apart: 18 -> 0, of which waited for: 15 -> 0; matrix products, arithmetic and copies ran while one was open for 83% -> 0% of each run, Pallas kernels for 0% -> 0%
where the time goes in v1:
time: 102 us
  Pallas kernels  95.6 us (94%)
  local copies, waits for them, and re-layouts  5.46 us (5%)
    pallas_call x1, Pallas kernels, local(): pl.pallas_call(kernel, out_shape=(jax.ShapeDtypeStruct((1, 1, 3, 2, B, B)...  95.6 us
    unnamed x10, local copies, waits for them, and re-layouts  5.46 us

profile of v1, /device:TPU:1, one launch (start us, length us, event | category | flops | bytes accessed | tf_op | source)
XLA Modules:
  0.0 101.7 jit_solution(3482755517783217306)
XLA Ops:
  0.6 0.0 copy-start
  0.6 1.1 %copy-done = f32[1,1,2,3,2,128,128]{6,5,4,3,2,1,0:T(8,128)S(1)} copy-done((f32[1,1,2,3,2,128,128]{6,5,4,3,2,1,0:T(8,128)S(1)}, f32[1,1,2,3,2,128,128]{6,5,4,3,2,1,0:T(8,128)}, u32[]{:S(2)}) %copy-start) | copy-done | bytes 786456
  1.8 0.0 copy-start.1
  1.8 0.9 copy-done.1
  2.7 0.0 copy-start.2
  2.7 0.9 copy-done.2
  3.6 0.0 copy-start.3
  3.6 0.9 copy-done.3
  4.5 95.6 %transport.1 = (f32[1,1,3,2,128,128]{5,4,3,2,1,0:T(8,128)S(1)}, f32[1,1,2,3,2,128,128]{6,5,4,3,2,1,0:T(8,128)S(1)}) custom-call(f32[1,2,128,128]{3,2,1,0:T(8,128)S(1)} %copy-done.1, f32[1,2,128,128]{3,2,1,0:T(8,128)S(1)} %copy-done.2, f32[1,1,2,128,128]{4,3,2,1,0:T(8,128)S(1)} %copy-done.3, f32[1,1,2,3,2,128,128]{6,5,4,3,2,1,0:T(8,128)S(1)} %copy-done), custom_call_target="tpu_custom_call" | custom-call | tf_op jit(solution)/shard_map/transport/pallas_call | solution.py:434
  100.1 0.7 copy.8
  100.8 0.9 copy.9
Async XLA Ops:
  0.6 1.1 %copy-start = (f32[1,1,2,3,2,128,128]{6,5,4,3,2,1,0:T(8,128)S(1)}, f32[1,1,2,3,2,128,128]{6,5,4,3,2,1,0:T(8,128)}, u32[]{:S(2)}) copy-start(f32[1,1,2,3,2,128,128]{6,5,4,3,2,1,0:T(8,128)} %screened.1) | copy-start | bytes 2359300
  1.8 0.9 copy-start.1
  2.7 0.9 copy-start.2
  3.6 0.9 copy-start.3

commit v2 on v1

--- a/solution.py
+++ b/solution.py
@@ -144,23 +144,36 @@
 
 def kernel(
     onsite, hopping, sigma, screened, green, out,
-    ahead, arrived, middle, outer, x, m, k1, k1h, k2, k2h, t, v, p, q2,
+    raw, c1, c1h, c2, c2h, c3, c3h, c4, c4h,
+    m, x, r, y, v, t, k, kp, w1, w1p, f, fp, base, pa, pb,
+    b_g0, b_g1, b_g2, b_a3, b_mo, b_k, b_kp, b_r, b_z,
     spectral, wbuf, dbuf, scaled, factor, sbuf,
-    s_hop, s_chain, s_mid, s_out, s_w, s_d, s_relay, s_sig,
-    r_hop, r_chain, r_mid, r_out, r_w, r_d, r_relay, r_sig,
+    s_mat, s_w, s_d, s_relay, s_sig,
+    r_raw, r_mat, r_w, r_d, r_relay, r_sig,
 ):
     e = lax.axis_index("energy")
     j = lax.axis_index("space")
     chip, core = e // 2, e % 2
     cx, cy = chip // 4, chip % 4
     left = j < NC // 2
-    is_mid = (j == NC // 2 - 1) | (j == NC // 2)
+    right = jnp.logical_not(left)
+    place = jnp.where(left, j, NC - 1 - j)
+    own = jnp.where(left, j, NC - j)
     row = pl.multiple_of(chip * 8, 8)
+
+    def at(p):
+        return jnp.where(left, p, NC - 1 - p)
 
     def relative(i):
         return ((cx + i // 4) % 4) * 4 + (cy + i % 4) % 4
 
     barrier = pltpu.get_barrier_semaphore()
+
+    def greet_z(i, c):
+        pl.semaphore_signal(
+            barrier, inc=1, device_id={"space": (j + i) % NC}, device_id_type=MESH
+        )
+        return c
 
     def greet(i, c):
         pl.semaphore_signal(
@@ -168,10 +181,7 @@
         )
         return c
 
-    for step in (1, NC - 1):
-        pl.semaphore_signal(
-            barrier, inc=1, device_id={"space": (j + step) % NC}, device_id_type=MESH
-        )
+    lax.fori_loop(1, NC, greet_z, 0)
     lax.fori_loop(1, NE, greet, 0)
 
     def energy_of(n, shape):
@@ -185,29 +195,8 @@
     m[0] = jnp.where(eye, en, 0.0) - 0.5 * (on_r + on_r.T) - sigma[0, 0, 0]
     m[1] = jnp.where(eye, BROADEN, 0.0) - 0.5 * (on_i - on_i.T) - sigma[0, 0, 1]
     hop = hopping.at[0]
-
-    @pl.when(left)
-    def _():
-        put(k1, hop)
-        put_dagger(k1h, hop)
-
-    @pl.when(jnp.logical_not(left))
-    def _():
-        put(k2h, hop)
-        put_dagger(k2, hop)
-
-    @pl.when(j == 0)
-    def _():
-        size = en * en + BROADEN * BROADEN
-        arrived[0] = jnp.where(eye, en / size, 0.0)
-        arrived[1] = jnp.where(eye, -BROADEN / size, 0.0)
-
-    @pl.when(j == NC - 1)
-    def _():
-        for ref in (arrived, k1, k1h):
-            ref[...] = jnp.zeros_like(ref)
-
-    pl.semaphore_wait(barrier, NE - 1 + 2)
+    g, u, w = green.at[0, 0, 0], green.at[0, 0, 1], green.at[0, 0, 2]
+    first = (place == 0) | (place == 2)
 
     def to_space(src, dst, s, r, where):
         return pltpu.make_async_remote_copy(
@@ -221,15 +210,67 @@
             device_id={"energy": where}, device_id_type=MESH,
         )
 
-    down = jnp.maximum(j - 1, 0)
-    up = jnp.minimum(j + 1, NC - 1)
-    inner = jnp.where(left, up, down)
-    outward = jnp.where(left, down, up)
-    hop_copy = to_space(hop, ahead, s_hop, r_hop, down)
-
-    @pl.when(j > 0)
-    def _():
-        hop_copy.start()
+    pending = []
+
+    def send(cond, src, dst, sem, where):
+        copy = to_space(src, dst, s_mat.at[len(pending)], r_mat.at[sem], where)
+        pending.append((cond, copy))
+        pl.when(cond)(copy.start)
+
+    def send_raw(cond, src, slot, where):
+        copy = to_space(src, raw.at[slot], s_mat.at[len(pending)], r_raw.at[slot], where)
+        pending.append((cond, copy))
+        pl.when(cond)(copy.start)
+
+    def have(ref, sem):
+        to_space(ref, ref, s_mat.at[0], r_mat.at[sem], j).wait_recv()
+
+    def have_raw(slot):
+        ref = raw.at[slot]
+        to_space(ref, ref, s_mat.at[0], r_raw.at[slot], j).wait_recv()
+
+    def coupling(c, ch, x):
+        xr, xi = x[0], x[1]
+        dr, di = xr.T, -xi.T
+        put(c, (jnp.where(left, xr, dr), jnp.where(left, xi, di)))
+        put(ch, (jnp.where(left, dr, xr), jnp.where(left, di, xi)))
+
+    def plus(a, b):
+        return a[0] + b[0], a[1] + b[1]
+
+    def minus(a, b):
+        return a[0] - b[0], a[1] - b[1]
+
+    pl.semaphore_wait(barrier, NE - 1 + NC - 1)
+
+    send_raw(left & (place == 1), hop, 1, 0)
+    send_raw(left & (place == 2), hop, 2, 1)
+    send_raw(left & (place == 3), hop, 3, 1)
+    send_raw(right & (place == 0), hop, 1, NC - 2)
+    send_raw(right & (place == 1), hop, 2, NC - 3)
+    send_raw(right & (place == 2), hop, 3, NC - 2)
+    send_raw(left & (place == 2), hop, 2, 3)
+    send_raw(left & (place == 3), hop, 3, 2)
+    send_raw(right & (place == 3), hop, 4, 3)
+
+    @pl.when(left & (place == 0))
+    def _():
+        size = en * en + BROADEN * BROADEN
+        zr, zi = en / size, -BROADEN / size
+        hr, hi = hop[0], hop[1]
+        put(v, (zr * hr - zi * hi, zr * hi + zi * hr))
+        hr, hi = hop[0].T, -hop[1].T
+        put(t, (zr * hr - zi * hi, zr * hi + zi * hr))
+        put(m, minus(m, mm(t, hop)))
+
+    @pl.when(first)
+    def _():
+        x[...] = m[...]
+        invert(x)
+
+    send(place == 0, x, b_g0, 0, at(1))
+    send(place == 2, x, b_g2, 2, at(1))
+    send(place == 2, x, b_g2, 2, at(3))
 
     def send_w(i, c):
         other = relative(i // 2)
@@ -243,93 +284,234 @@
     lax.fori_loop(1, NE, send_w, 0)
     wbuf[e] = screened[0, 0, core, :, :, pl.ds(row, 8), :]
 
-    @pl.when(jnp.logical_not(left) & (j < NC - 1))
-    def _():
-        hop_copy.wait_recv()
-        put(k1h, ahead)
-        put_dagger(k1, ahead)
-
     def occupations(n, c):
         f = 1.0 / (1.0 + jnp.exp(energy_of(n, (8, B)) / THERMAL))
         factor[n] = jnp.where(jnp.full((8, B), core, jnp.int32) == 0, -f, 1.0 - f)
         return c
 
-    chain = to_space(x, arrived, s_chain, r_chain, inner)
-    meet = to_space(x, middle, s_mid, r_mid, inner)
-
-    @pl.when((j > 0) & (j < NC - 1))
-    def _():
-        chain.wait_recv()
-
-    put(t, mm(k1h, arrived))
-    sr, si = mm(t, k1)
-    m[0] = m[0] - sr
-    m[1] = m[1] - si
-    x[...] = m[...]
-    invert(x)
-
-    @pl.when(jnp.logical_not(is_mid))
-    def _():
-        chain.start()
-
-    @pl.when(is_mid)
-    def _():
-        meet.start()
-
-    lax.fori_loop(0, NE, occupations, 0)
-    for n in range(8):
-        scaled[n] = jnp.zeros_like(scaled[n])
-
-    @pl.when(left)
-    def _():
-        hop_copy.wait_recv()
-        put(k2, ahead)
-        put_dagger(k2h, ahead)
-        put(v, mm(arrived, k1))
-
-    g = green.at[0, 0, 0]
-    onward = to_space(g, outer, s_out, r_out, outward)
-
-    @pl.when(is_mid)
-    def _():
-        meet.wait_recv()
-        ar, ai = mm(k2, middle)
-        sr, si = product(ar, ai, k2h[0], k2h[1])
-        g[0] = m[0] - sr
-        g[1] = m[1] - si
-        invert(g)
-        onward.start()
-
-        @pl.when(j == NC // 2)
-        def _():
-            put(t, (ar, ai))
-            put(v, mm(middle, k2h))
-
-    @pl.when(jnp.logical_not(is_mid))
-    def _():
-        put(p, mm(x, k2))
-        put(q2, mm(k2h, x))
-        onward.wait_recv()
-        put(m, mm(p, outer))
-        ar, ai = mm(m, q2)
-        g[0] = x[0] + ar
-        g[1] = x[1] + ai
-
-        @pl.when((j > 0) & (j < NC - 1))
-        def _():
-            onward.start()
-
-    @pl.when(j <= NC // 2)
-    def _():
-        put(green.at[0, 0, 1], mm(v, g))
-        put(green.at[0, 0, 2], mm(g, t))
-
-    @pl.when(j > NC // 2)
-    def _():
-        put(green.at[0, 0, 1], mm(outer, q2))
-        put(green.at[0, 0, 2], (m[0], m[1]))
-
-    u, w = green.at[0, 0, 1], green.at[0, 0, 2]
+    @pl.when(place != 1)
+    def _():
+        lax.fori_loop(0, NE, occupations, 0)
+        for n in range(8):
+            scaled[n] = jnp.zeros_like(scaled[n])
+
+    @pl.when(place == 3)
+    def _():
+        have(b_g2, 2)
+
+    @pl.when(left & (place == 3))
+    def _():
+        have_raw(4)
+
+    send(place == 3, m, b_a3, 3, at(1))
+    send_raw(left & (place == 3), raw.at[4], 4, 1)
+    send_raw(right & (place == 3), hop, 4, NC - 2)
+
+    @pl.when(place == 1)
+    def _():
+        @pl.when(left)
+        def _():
+            coupling(c1, c1h, hop)
+            have_raw(2)
+            coupling(c2, c2h, raw.at[2])
+
+        @pl.when(right)
+        def _():
+            coupling(c2, c2h, hop)
+            have_raw(1)
+            coupling(c1, c1h, raw.at[1])
+
+        lax.fori_loop(0, NE, occupations, 0)
+        for n in range(8):
+            scaled[n] = jnp.zeros_like(scaled[n])
+        have_raw(3)
+        coupling(c3, c3h, raw.at[3])
+        have(b_g2, 2)
+        put(pa, mm(b_g2, c3))
+        put(k, mm(c2, pa))
+        put(kp, mm(c3h, b_g2))
+        put(kp, mm(kp, c2h))
+        put(base, mm(c3h, pa))
+        put(pb, mm(c2, b_g2))
+        put(m, minus(m, mm(pb, c2h)))
+        have(b_g0, 0)
+        put(t, mm(c1h, b_g0))
+        put(m, minus(m, mm(t, c1)))
+
+    send(place == 1, k, b_k, 5, at(0))
+    send(place == 1, kp, b_kp, 6, at(0))
+
+    @pl.when(place == 1)
+    def _():
+        x[...] = m[...]
+        invert(x)
+        put(w1, mm(x, k))
+        put(y, mm(kp, w1))
+        have(b_a3, 3)
+        put(r, minus(minus(b_a3, base), y))
+        m[...] = r[...]
+
+    send(place == 1, m, b_mo, 4, NC - 1 - j)
+    send(place == 1, x, b_g1, 1, at(2))
+    send(left & (place == 1), x, b_g1, 1, 3)
+    send(place == 1, x, b_g1, 1, at(0))
+
+    @pl.when(place == 1)
+    def _():
+        invert(r)
+
+    send(right & (place == 1), r, b_r, 7, NC // 2)
+
+    @pl.when(place == 1)
+    def _():
+        have_raw(4)
+        coupling(c4, c4h, raw.at[4])
+        put(pa, mm(r, c4))
+        put(pb, mm(c4h, pa))
+        put(base, mm(c4h, r))
+        have(b_mo, 4)
+        put(y, minus(b_mo, pb))
+        invert(y)
+
+    send(right & (place == 1), y, b_z, 8, NC // 2)
+
+    @pl.when(place == 1)
+    def _():
+        put(pb, mm(pa, y))
+        put(b_z, plus(r, mm(pb, base)))
+
+    send(left & (place == 1), b_z, b_z, 8, 3)
+    send(place == 1, b_z, b_z, 8, at(2))
+    send(place == 1, b_z, b_z, 8, at(0))
+
+    @pl.when(place == 1)
+    def _():
+        put(w1p, mm(kp, x))
+        put(f, mm(w1, b_z))
+        put(g, plus(x, mm(f, w1p)))
+
+        @pl.when(left)
+        def _():
+            put(v, mm(b_g0, c1))
+            put(u, mm(v, g))
+            put(w, mm(g, t))
+
+        @pl.when(right)
+        def _():
+            put(pa, mm(b_z, w1p))
+            put(pa, plus(mm(c2h, g), mm(c3, pa)))
+            put(u, mm(b_g2, pa))
+            put(pb, plus(mm(g, c2), mm(f, c3h)))
+            put(w, mm(pb, b_g2))
+
+    @pl.when(place == 0)
+    def _():
+        @pl.when(left)
+        def _():
+            have_raw(1)
+            coupling(c1, c1h, raw.at[1])
+
+        @pl.when(right)
+        def _():
+            coupling(c1, c1h, hop)
+
+        put(pa, mm(x, c1))
+        put(pb, mm(c1h, x))
+        have(b_k, 5)
+        have(b_kp, 6)
+        have(b_g1, 1)
+        put(w1, mm(b_g1, b_k))
+        put(w1p, mm(b_kp, b_g1))
+        put(f, mm(pa, w1))
+        put(fp, mm(w1p, pb))
+        put(k, mm(pa, b_g1))
+        put(kp, mm(b_g1, pb))
+        put(base, plus(x, mm(k, pb)))
+        have(b_z, 8)
+        put(y, mm(b_z, fp))
+        put(g, plus(base, mm(f, y)))
+
+        @pl.when(left)
+        def _():
+            put(u, mm(v, g))
+            put(w, mm(g, t))
+
+        @pl.when(right)
+        def _():
+            put(u, plus(kp, mm(w1, y)))
+            put(r, mm(f, b_z))
+            put(w, plus(k, mm(r, w1p)))
+
+    def prepare(g2):
+        put(pa, mm(g2, c3))
+        put(k, mm(c2, pa))
+        put(pb, mm(c3h, g2))
+        put(kp, mm(pb, c2h))
+        have(b_g1, 1)
+        put(w1, mm(b_g1, k))
+        put(w1p, mm(kp, b_g1))
+        put(pa, plus(c3, mm(c2h, w1)))
+        put(f, mm(g2, pa))
+        put(pb, plus(c3h, mm(w1p, c2)))
+        put(fp, mm(pb, g2))
+
+    @pl.when(place == 2)
+    def _():
+        @pl.when(left)
+        def _():
+            coupling(c2, c2h, hop)
+            have_raw(3)
+            coupling(c3, c3h, raw.at[3])
+
+        @pl.when(right)
+        def _():
+            coupling(c3, c3h, hop)
+            have_raw(2)
+            coupling(c2, c2h, raw.at[2])
+
+        prepare(x)
+        put(pa, mm(x, c2h))
+        put(pb, mm(c2, x))
+        put(k, mm(pa, b_g1))
+        put(kp, mm(b_g1, pb))
+        put(base, plus(x, mm(k, pb)))
+        have(b_z, 8)
+        put(y, mm(b_z, fp))
+        put(g, plus(base, mm(f, y)))
+        put(r, mm(f, b_z))
+
+        @pl.when(left)
+        def _():
+            put(u, plus(kp, mm(w1, y)))
+            put(w, plus(k, mm(r, w1p)))
+
+        @pl.when(right)
+        def _():
+            put(u, (y[0], y[1]))
+            put(w, (r[0], r[1]))
+
+    @pl.when(left & (place == 3))
+    def _():
+        coupling(c3, c3h, hop)
+        have_raw(2)
+        coupling(c2, c2h, raw.at[2])
+        prepare(b_g2)
+        have(b_z, 8)
+        put(g, (b_z[0], b_z[1]))
+        put(u, mm(f, b_z))
+        put(w, mm(b_z, fp))
+
+    @pl.when(right & (place == 3))
+    def _():
+        coupling(c4, c4h, hop)
+        have(b_r, 7)
+        put(pa, mm(b_r, c4))
+        put(pb, mm(c4h, b_r))
+        have(b_z, 8)
+        put(w, mm(pa, b_z))
+        put(g, plus(b_r, mm(w, pb)))
+        put(u, mm(b_z, pb))
+
     spectral[0, 0] = g[0] - g[0].T
     spectral[0, 1] = g[1] + g[1].T
     dr = u[0] - w[0].T
@@ -405,21 +587,8 @@
     lax.fori_loop(0, 4, convolve, 0)
     out[0, 0, core, :, :, pl.ds(row, 8), :] = sbuf[e]
 
-    @pl.when(j > 0)
-    def _():
-        hop_copy.wait_send()
-
-    @pl.when(jnp.logical_not(is_mid))
-    def _():
-        chain.wait_send()
-
-    @pl.when(is_mid)
-    def _():
-        meet.wait_send()
-
-    @pl.when((j > 0) & (j < NC - 1))
-    def _():
-        onward.wait_send()
+    for cond, copy in pending:
+        pl.when(cond)(copy.wait_send)
 
     to_energy(many, many, s_w, r_w, e).wait_send()
     to_energy(some, some, s_d, r_d, e).wait_send()
@@ -439,7 +608,8 @@
         ),
         in_specs=[vmem] * 4,
         out_specs=(vmem, vmem),
-        scratch_shapes=[square] * 14
+        scratch_shapes=[pltpu.VMEM((5, 2, B, B), F32)]
+        + [square] * 32
         + [
             pltpu.VMEM((3, 2, B, B), F32),
             pltpu.VMEM((NE, 3, 2, 8, B), F32),
@@ -448,7 +618,10 @@
             pltpu.VMEM((NE, 8, B), F32),
             pltpu.VMEM((NE, 3, 2, 8, B), F32),
         ]
-        + [pltpu.SemaphoreType.DMA] * 16,
+        + [pltpu.SemaphoreType.DMA((32,))]
+        + [pltpu.SemaphoreType.DMA] * 4
+        + [pltpu.SemaphoreType.DMA((5,)), pltpu.SemaphoreType.DMA((9,))]
+        + [pltpu.SemaphoreType.DMA] * 4,
         compiler_params=pltpu.CompilerParams(
             collective_id=0, has_side_effects=True, vmem_limit_bytes=48 * 2**20
         ),

time: 102 us -> 75.6 us (0.74)
  Pallas kernels: 95.6 us -> 69.3 us
    pallas_call x1, Pallas kernels: 95.6 us -> 69.3 us  [local(): pl.pallas_call(kernel, out_shape=(jax.ShapeDtypeStruct((1, 1, 3, 2, B, B)...]
where the time goes in v2:
time: 75.6 us; the launch traced here: 75.4 us
  Pallas kernels  69.3 us (92%)
  local copies, waits for them, and re-layouts  5.46 us (7%)
    pallas_call x1, Pallas kernels, local(): pl.pallas_call(kernel, out_shape=(jax.ShapeDtypeStruct((1, 1, 3, 2, B, B)...  69.3 us
    unnamed x10, local copies, waits for them, and re-layouts  5.46 us

profile of v2, /device:TPU:1, one launch (start us, length us, event | category | flops | bytes accessed | tf_op | source)
XLA Modules:
  0.0 75.4 jit_solution(8257681643839749463)
XLA Ops:
  0.6 0.0 copy-start
  0.6 1.1 %copy-done = f32[1,1,2,3,2,128,128]{6,5,4,3,2,1,0:T(8,128)S(1)} copy-done((f32[1,1,2,3,2,128,128]{6,5,4,3,2,1,0:T(8,128)S(1)}, f32[1,1,2,3,2,128,128]{6,5,4,3,2,1,0:T(8,128)}, u32[]{:S(2)}) %copy-start) | copy-done | bytes 786456
  1.8 0.0 copy-start.1
  1.8 0.9 %copy-done.1 = f32[1,2,128,128]{3,2,1,0:T(8,128)S(1)} copy-done((f32[1,2,128,128]{3,2,1,0:T(8,128)S(1)}, f32[1,2,128,128]{3,2,1,0:T(8,128)}, u32[]{:S(2)}) %copy-start.1) | copy-done | bytes 131096
  2.7 0.0 copy-start.2
  2.7 0.9 %copy-done.2 = f32[1,2,128,128]{3,2,1,0:T(8,128)S(1)} copy-done((f32[1,2,128,128]{3,2,1,0:T(8,128)S(1)}, f32[1,2,128,128]{3,2,1,0:T(8,128)}, u32[]{:S(2)}) %copy-start.2) | copy-done | bytes 131096
  3.6 0.0 copy-start.3
  3.6 0.9 %copy-done.3 = f32[1,1,2,128,128]{4,3,2,1,0:T(8,128)S(1)} copy-done((f32[1,1,2,128,128]{4,3,2,1,0:T(8,128)S(1)}, f32[1,1,2,128,128]{4,3,2,1,0:T(8,128)}, u32[]{:S(2)}) %copy-start.3) | copy-done | bytes 131096
  4.5 69.3 %transport.1 = (f32[1,1,3,2,128,128]{5,4,3,2,1,0:T(8,128)S(1)}, f32[1,1,2,3,2,128,128]{6,5,4,3,2,1,0:T(8,128)S(1)}) custom-call(f32[1,2,128,128]{3,2,1,0:T(8,128)S(1)} %copy-done.1, f32[1,2,128,128]{3,2,1,0:T(8,128)S(1)} %copy-done.2, f32[1,1,2,128,128]{4,3,2,1,0:T(8,128)S(1)} %copy-done.3, f32[1,1,2,3,2,128,128]{6,5,4,3,2,1,0:T(8,128)S(1)} %copy-done), custom_call_target="tpu_custom_call" | custom-call | tf_op jit(solution)/shard_map/transport/pallas_call | solution.py:603
  73.8 0.7 copy.8
  74.5 0.9 %copy.9 = f32[1,1,2,3,2,128,128]{6,5,4,3,2,1,0:T(8,128)} copy(f32[1,1,2,3,2,128,128]{6,5,4,3,2,1,0:T(8,128)S(1)} %get-tuple-element.5) | data formatting | bytes 1572864
Async XLA Ops:
  0.6 1.1 %copy-start = (f32[1,1,2,3,2,128,128]{6,5,4,3,2,1,0:T(8,128)S(1)}, f32[1,1,2,3,2,128,128]{6,5,4,3,2,1,0:T(8,128)}, u32[]{:S(2)}) copy-start(f32[1,1,2,3,2,128,128]{6,5,4,3,2,1,0:T(8,128)} %screened.1) | copy-start | bytes 2359300
  1.8 0.9 %copy-start.1 = (f32[1,2,128,128]{3,2,1,0:T(8,128)S(1)}, f32[1,2,128,128]{3,2,1,0:T(8,128)}, u32[]{:S(2)}) copy-start(f32[1,2,128,128]{3,2,1,0:T(8,128)} %onsite.1) | copy-start | bytes 393220
  2.7 0.9 %copy-start.2 = (f32[1,2,128,128]{3,2,1,0:T(8,128)S(1)}, f32[1,2,128,128]{3,2,1,0:T(8,128)}, u32[]{:S(2)}) copy-start(f32[1,2,128,128]{3,2,1,0:T(8,128)} %hopping.1) | copy-start | bytes 393220
  3.6 0.9 %copy-start.3 = (f32[1,1,2,128,128]{4,3,2,1,0:T(8,128)S(1)}, f32[1,1,2,128,128]{4,3,2,1,0:T(8,128)}, u32[]{:S(2)}) copy-start(f32[1,1,2,128,128]{4,3,2,1,0:T(8,128)} %sigma.1) | copy-start | bytes 393220

commit v3 on v2

--- a/solution.py
+++ b/solution.py
@@ -49,41 +49,66 @@
     ref[1] = -x[1].T
 
 
+def times(a, b):
+    return a[0] * b[0] - a[1] * b[1], a[0] * b[1] + a[1] * b[0]
+
+
+def plus(a, b):
+    return a[0] + b[0], a[1] + b[1]
+
+
+def minus(a, b):
+    return a[0] - b[0], a[1] - b[1]
+
+
+def choose(cond, a, b):
+    return jnp.where(cond, a[0], b[0]), jnp.where(cond, a[1], b[1])
+
+
+def negative(a):
+    return -a[0], -a[1]
+
+
 def tile_inverse(tr, ti, off, lane, sub):
     shape = tr.shape
+
+    def spread(x, k):
+        return tuple(jnp.broadcast_to(part[k : k + 1], shape) for part in x)
+
     cols = [
-        (
-            jnp.broadcast_to(tr[:, off + j : off + j + 1], shape),
-            jnp.broadcast_to(ti[:, off + j : off + j + 1], shape),
-        )
+        tuple(jnp.broadcast_to(part[:, off + j : off + j + 1], shape) for part in (tr, ti))
         for j in range(8)
     ]
-    for k in range(8):
-        cr, ci = cols[k]
-        pr = jnp.broadcast_to(cr[k : k + 1], shape)
-        pi = jnp.broadcast_to(ci[k : k + 1], shape)
-        inv = 1.0 / (pr * pr + pi * pi)
-        qr = pr * inv
-        qi = -(pi * inv)
-        own = sub == k
-        mr = jnp.where(own, -qr, cr * qr - ci * qi)
-        mi = jnp.where(own, -qi, cr * qi + ci * qr)
-
-        def step(xr, xi):
-            br = jnp.broadcast_to(xr[k : k + 1], shape)
-            bi = jnp.broadcast_to(xi[k : k + 1], shape)
-            return (
-                jnp.where(own, 0.0, xr) - (mr * br - mi * bi),
-                jnp.where(own, 0.0, xi) - (mr * bi + mi * br),
+    rows = (tr, ti)
+    for k in range(0, 8, 2):
+        c0, c1 = cols[k], cols[k + 1]
+        a, b, c, d = spread(c0, k), spread(c1, k), spread(c0, k + 1), spread(c1, k + 1)
+        det = minus(times(a, d), times(b, c))
+        own0, own1 = sub == k, sub == k + 1
+        either = own0 | own1
+        n0 = minus(times(c0, d), times(c1, c))
+        n1 = minus(times(c1, a), times(c0, b))
+        n0 = choose(own0, negative(d), choose(own1, c, n0))
+        n1 = choose(own0, b, choose(own1, negative(a), n1))
+        inv = 1.0 / (det[0] * det[0] + det[1] * det[1])
+        q = (det[0] * inv, -(det[1] * inv))
+        m0, m1 = times(n0, q), times(n1, q)
+
+        def step(x):
+            keep = tuple(jnp.where(either, 0.0, part) for part in x)
+            return minus(keep, plus(times(m0, spread(x, k)), times(m1, spread(x, k + 1))))
+
+        for j in range(k + 2, 8):
+            cols[j] = step(cols[j])
+        h0, h1 = lane == off + k, lane == off + k + 1
+        unit0, unit1 = jnp.where(own0, 1.0, 0.0), jnp.where(own1, 1.0, 0.0)
+        rows = step(
+            (
+                jnp.where(h0, unit0, jnp.where(h1, unit1, rows[0])),
+                jnp.where(h0 | h1, 0.0, rows[1]),
             )
-
-        for j in range(k + 1, 8):
-            cols[j] = step(*cols[j])
-        here = lane == off + k
-        tr, ti = step(
-            jnp.where(here, jnp.where(own, 1.0, 0.0), tr), jnp.where(here, 0.0, ti)
         )
-    return tr, ti
+    return rows
 
 
 def panel_inverse(pr, pi):
@@ -113,42 +138,78 @@
 
 
 def invert(x):
-    rest, back = B - PANEL, B - PANEL
+    rest = B - PANEL
     lane = lax.broadcasted_iota(jnp.int32, (rest, B), 1)
 
-    def body(_, panel):
-        xr, xi = x[0, PANEL:, :], x[1, PANEL:, :]
-        columns = jnp.concatenate([xr[:, :PANEL], xi[:, :PANEL]], axis=1)
-        ch, cl = split(columns)
-        x[0, :rest, :] = pltpu.roll(jnp.where(lane < PANEL, 0.0, xr), back, 1)
-        x[1, :rest, :] = pltpu.roll(jnp.where(lane < PANEL, 0.0, xi), back, 1)
-        rr, ri = panel_inverse(*panel)
-        rr, ri = pltpu.roll(rr, back, 1), pltpu.roll(ri, back, 1)
-        rows = jnp.concatenate(
-            [jnp.concatenate([rr, ri], axis=1), jnp.concatenate([-ri, rr], axis=1)], axis=0
+    def turned(part):
+        return pltpu.roll(part, rest, 1)
+
+    def body(_, carry):
+        pr, pi, columns, rows = carry
+        update = dot(columns, rows)
+        xr = x[0, PANEL:, :] - update[:, :B]
+        xi = x[1, PANEL:, :] - update[:, B:]
+        ch, cl = split(jnp.concatenate([xr[:, :PANEL], xi[:, :PANEL]], axis=1))
+        columns = jnp.concatenate([ch, ch, cl], axis=1)
+        zr = turned(jnp.where(lane < PANEL, 0.0, xr))
+        zi = turned(jnp.where(lane < PANEL, 0.0, xi))
+        rr, ri = panel_inverse(pr, pi)
+        rr, ri = turned(rr), turned(ri)
+        rh, rl = split(
+            jnp.concatenate(
+                [jnp.concatenate([rr, ri], axis=1), jnp.concatenate([-ri, rr], axis=1)],
+                axis=0,
+            )
         )
-        rh, rl = split(rows)
-        update = dot(
-            jnp.concatenate([ch, ch, cl], axis=1), jnp.concatenate([rh, rl, rh], axis=0)
-        )
-        nr = x[0, :rest, :] - update[:, :B]
-        ni = x[1, :rest, :] - update[:, B:]
-        x[0, :rest, :] = nr
-        x[1, :rest, :] = ni
+        rows = jnp.concatenate([rh, rl, rh], axis=0)
+        new = []
+        for t in range(0, PANEL, 8):
+            total = (jnp.zeros((8, B), F32), jnp.zeros((8, B), F32))
+            for q in range(PANEL):
+                col = tuple(
+                    jnp.broadcast_to(part[t : t + 8, q : q + 1], (8, B)) for part in (xr, xi)
+                )
+                row = tuple(jnp.broadcast_to(part[q : q + 1], (8, B)) for part in (rr, ri))
+                total = plus(total, times(col, row))
+            new.append(minus((zr[t : t + 8], zi[t : t + 8]), total))
+        x[0, PANEL:rest, :] = zr[PANEL:]
+        x[1, PANEL:rest, :] = zi[PANEL:]
         x[0, rest:, :] = rr
         x[1, rest:, :] = ri
-        return nr[:PANEL], ni[:PANEL]
-
-    lax.fori_loop(0, B // PANEL, body, (x[0, :PANEL, :], x[1, :PANEL, :]))
+        done = jnp.zeros((PANEL, columns.shape[1]), columns.dtype)
+        return (
+            jnp.concatenate([part[0] for part in new]),
+            jnp.concatenate([part[1] for part in new]),
+            jnp.concatenate([columns[PANEL:], done]),
+            rows,
+        )
+
+    pr, pi, columns, rows = lax.fori_loop(
+        0,
+        B // PANEL,
+        body,
+        (
+            x[0, :PANEL, :],
+            x[1, :PANEL, :],
+            jnp.zeros((rest, 6 * PANEL), jnp.bfloat16),
+            jnp.zeros((6 * PANEL, 2 * B), jnp.bfloat16),
+        ),
+    )
+    update = dot(columns, rows)
+    x[0, PANEL:, :] = x[0, PANEL:, :] - update[:, :B]
+    x[1, PANEL:, :] = x[1, PANEL:, :] - update[:, B:]
+    x[0, :PANEL, :] = pr
+    x[1, :PANEL, :] = pi
 
 
 def kernel(
-    onsite, hopping, sigma, screened, green, out,
+    onsite_in, hopping_in, sigma_in, screened, green, out,
+    onsite, hop, sigma,
     raw, c1, c1h, c2, c2h, c3, c3h, c4, c4h,
     m, x, r, y, v, t, k, kp, w1, w1p, f, fp, base, pa, pb,
     b_g0, b_g1, b_g2, b_a3, b_mo, b_k, b_kp, b_r, b_z,
     spectral, wbuf, dbuf, scaled, factor, sbuf,
-    s_mat, s_w, s_d, s_relay, s_sig,
+    s_in, s_mat, s_w, s_d, s_relay, s_sig,
     r_raw, r_mat, r_w, r_d, r_relay, r_sig,
 ):
     e = lax.axis_index("energy")
@@ -167,6 +228,17 @@
     def relative(i):
         return ((cx + i // 4) % 4) * 4 + (cy + i % 4) % 4
 
+    loads = [
+        pltpu.make_async_copy(onsite_in.at[0], onsite, s_in.at[0]),
+        pltpu.make_async_copy(sigma_in.at[0, 0], sigma, s_in.at[1]),
+        pltpu.make_async_copy(hopping_in.at[0], hop, s_in.at[2]),
+    ]
+    for load in loads:
+        load.start()
+    own_w = pltpu.make_async_copy(
+        screened.at[0, 0, core, :, :, pl.ds(row, 8), :], wbuf.at[e], s_in.at[3]
+    )
+    own_w.start()
     barrier = pltpu.get_barrier_semaphore()
 
     def greet_z(i, c):
@@ -191,10 +263,11 @@
         jnp.int32, (B, B), 1
     )
     en = energy_of(e, (B, B))
-    on_r, on_i = onsite[0, 0], onsite[0, 1]
-    m[0] = jnp.where(eye, en, 0.0) - 0.5 * (on_r + on_r.T) - sigma[0, 0, 0]
-    m[1] = jnp.where(eye, BROADEN, 0.0) - 0.5 * (on_i - on_i.T) - sigma[0, 0, 1]
-    hop = hopping.at[0]
+    for load in loads:
+        load.wait()
+    on_r, on_i = onsite[0], onsite[1]
+    m[0] = jnp.where(eye, en, 0.0) - 0.5 * (on_r + on_r.T) - sigma[0]
+    m[1] = jnp.where(eye, BROADEN, 0.0) - 0.5 * (on_i - on_i.T) - sigma[1]
     g, u, w = green.at[0, 0, 0], green.at[0, 0, 1], green.at[0, 0, 2]
     first = (place == 0) | (place == 2)
 
@@ -234,12 +307,6 @@
         dr, di = xr.T, -xi.T
         put(c, (jnp.where(left, xr, dr), jnp.where(left, xi, di)))
         put(ch, (jnp.where(left, dr, xr), jnp.where(left, di, xi)))
-
-    def plus(a, b):
-        return a[0] + b[0], a[1] + b[1]
-
-    def minus(a, b):
-        return a[0] - b[0], a[1] - b[1]
 
     pl.semaphore_wait(barrier, NE - 1 + NC - 1)
 
@@ -282,7 +349,6 @@
         return c
 
     lax.fori_loop(1, NE, send_w, 0)
-    wbuf[e] = screened[0, 0, core, :, :, pl.ds(row, 8), :]
 
     def occupations(n, c):
         f = 1.0 / (1.0 + jnp.exp(energy_of(n, (8, B)) / THERMAL))
@@ -358,14 +424,14 @@
 
     @pl.when(place == 1)
     def _():
-        invert(r)
-
-    send(right & (place == 1), r, b_r, 7, NC // 2)
-
-    @pl.when(place == 1)
-    def _():
         have_raw(4)
         coupling(c4, c4h, raw.at[4])
+        invert(r)
+
+    send(right & (place == 1), r, b_r, 7, NC // 2)
+
+    @pl.when(place == 1)
+    def _():
         put(pa, mm(r, c4))
         put(pb, mm(c4h, pa))
         put(base, mm(c4h, r))
@@ -380,8 +446,8 @@
         put(pb, mm(pa, y))
         put(b_z, plus(r, mm(pb, base)))
 
+    send(place == 1, b_z, b_z, 8, at(2))
     send(left & (place == 1), b_z, b_z, 8, 3)
-    send(place == 1, b_z, b_z, 8, at(2))
     send(place == 1, b_z, b_z, 8, at(0))
 
     @pl.when(place == 1)
@@ -427,17 +493,25 @@
         put(k, mm(pa, b_g1))
         put(kp, mm(b_g1, pb))
         put(base, plus(x, mm(k, pb)))
-        have(b_z, 8)
-        put(y, mm(b_z, fp))
-        put(g, plus(base, mm(f, y)))
 
         @pl.when(left)
         def _():
-            put(u, mm(v, g))
-            put(w, mm(g, t))
+            put(c2, mm(v, base))
+            put(c2h, mm(v, f))
+            put(c3, mm(base, t))
+            put(c3h, mm(fp, t))
+            have(b_z, 8)
+            put(y, mm(b_z, fp))
+            put(r, mm(b_z, c3h))
+            put(g, plus(base, mm(f, y)))
+            put(u, plus(c2, mm(c2h, y)))
+            put(w, plus(c3, mm(f, r)))
 
         @pl.when(right)
         def _():
+            have(b_z, 8)
+            put(y, mm(b_z, fp))
+            put(g, plus(base, mm(f, y)))
             put(u, plus(kp, mm(w1, y)))
             put(r, mm(f, b_z))
             put(w, plus(k, mm(r, w1p)))
@@ -521,21 +595,30 @@
     spectral[2, 0] = -dr.T
     spectral[2, 1] = di.T
 
-    def send_d(i, c):
+    near = sorted(range(1, NE // 2), key=lambda i: min(i // 4, 4 - i // 4) + min(i % 4, 4 - i % 4))
+    for i in near[::-1]:
         other = relative(i)
         to_energy(
             spectral.at[:, :, pl.ds(pl.multiple_of(other * 8, 8), 8), :],
-            dbuf.at[core, chip], s_d, r_d, other * 2 + core,
+            dbuf.at[core, chip], s_d, r_d.at[i], other * 2 + core,
         ).start()
-        return c
-
-    lax.fori_loop(1, NE // 2, send_d, 0)
     dbuf[core, chip] = spectral[:, :, pl.ds(row, 8), :]
+    sibling = chip * 2 + 1 - core
+
+    def pass_on(source):
+        piece = dbuf.at[core, source]
+        to_energy(piece, piece, s_relay, r_relay, sibling).start()
+
+    for i in near:
+        source = ((cx + 4 - i // 4) % 4) * 4 + (cy + 4 - i % 4) % 4
+        piece = dbuf.at[core, source]
+        to_energy(piece, piece, s_d, r_d.at[i], e).wait_recv()
+        pass_on(source)
+    pass_on(chip)
     some = dbuf.at[0, pl.ds(0, NE // 2 - 1)]
-    to_energy(some, some, s_d, r_d, e).wait_recv()
-    relay = to_energy(dbuf.at[core], dbuf.at[core], s_relay, r_relay, chip * 2 + 1 - core)
-    relay.start()
+    relay = to_energy(dbuf.at[0], dbuf.at[0], s_relay, r_relay, sibling)
     many = wbuf.at[pl.ds(0, NE - 1)]
+    own_w.wait()
     to_energy(many, many, s_w, r_w, e).wait_recv()
     relay.wait_recv()
 
@@ -591,7 +674,7 @@
         pl.when(cond)(copy.wait_send)
 
     to_energy(many, many, s_w, r_w, e).wait_send()
-    to_energy(some, some, s_d, r_d, e).wait_send()
+    to_energy(some, some, s_d, r_d.at[0], e).wait_send()
     relay.wait_send()
     to_energy(many, many, s_sig, r_sig, e).wait_send()
     to_energy(many, many, s_sig, r_sig, e).wait_recv()
@@ -599,6 +682,7 @@
 
 def local(onsite, hopping, sigma_old, screened):
     vmem = pl.BlockSpec(memory_space=pltpu.VMEM)
+    hbm = pl.BlockSpec(memory_space=pltpu.HBM)
     square = pltpu.VMEM((2, B, B), F32)
     return pl.pallas_call(
         kernel,
@@ -606,9 +690,10 @@
             jax.ShapeDtypeStruct((1, 1, 3, 2, B, B), F32),
             jax.ShapeDtypeStruct((1, 1, 2, 3, 2, B, B), F32),
         ),
-        in_specs=[vmem] * 4,
+        in_specs=[hbm] * 4,
         out_specs=(vmem, vmem),
-        scratch_shapes=[pltpu.VMEM((5, 2, B, B), F32)]
+        scratch_shapes=[square] * 3
+        + [pltpu.VMEM((5, 2, B, B), F32)]
         + [square] * 32
         + [
             pltpu.VMEM((3, 2, B, B), F32),
@@ -618,15 +703,16 @@
             pltpu.VMEM((NE, 8, B), F32),
             pltpu.VMEM((NE, 3, 2, 8, B), F32),
         ]
-        + [pltpu.SemaphoreType.DMA((32,))]
+        + [pltpu.SemaphoreType.DMA((4,)), pltpu.SemaphoreType.DMA((32,))]
         + [pltpu.SemaphoreType.DMA] * 4
         + [pltpu.SemaphoreType.DMA((5,)), pltpu.SemaphoreType.DMA((9,))]
-        + [pltpu.SemaphoreType.DMA] * 4,
+        + [pltpu.SemaphoreType.DMA, pltpu.SemaphoreType.DMA((NE // 2,))]
+        + [pltpu.SemaphoreType.DMA] * 2,
         compiler_params=pltpu.CompilerParams(
             collective_id=0, has_side_effects=True, vmem_limit_bytes=48 * 2**20
         ),
         name="transport",
-    )(onsite, hopping, sigma_old, screened)
+    )(*(pltpu.with_memory_space_constraint(a, pltpu.HBM) for a in (onsite, hopping, sigma_old, screened)))
 
 
 def solution(mesh):

time: 75.6 us -> 68.9 us (0.911)
  local copies, waits for them, and re-layouts: 5.46 us -> 1.63 us
  Pallas kernels: 69.3 us -> 66.6 us
    unnamed x10 -> x2, local copies, waits for them, and re-layouts: 5.46 us -> 1.63 us
    pallas_call x1, Pallas kernels: 69.3 us -> 66.6 us  [local(): pl.pallas_call(kernel, out_shape=(jax.ShapeDtypeStruct((1, 1, 3, 2, B, B)...]
where the time goes in v3:
time: 68.9 us; the launch traced here: 68.8 us
  Pallas kernels  66.6 us (97%)
  local copies, waits for them, and re-layouts  1.63 us (2%)
    pallas_call x1, Pallas kernels, local(): pl.pallas_call(kernel, out_shape=(jax.ShapeDtypeStruct((1, 1, 3, 2, B, B)...  66.6 us
    unnamed x2, local copies, waits for them, and re-layouts  1.63 us

profile of v3, /device:TPU:1, one launch (start us, length us, event | category | flops | bytes accessed | tf_op | source)
XLA Modules:
  0.0 68.8 jit_solution(10739785329277744964)
XLA Ops:
  0.6 66.6 %transport.1 = (f32[1,1,3,2,128,128]{5,4,3,2,1,0:T(8,128)S(1)}, f32[1,1,2,3,2,128,128]{6,5,4,3,2,1,0:T(8,128)S(1)}) custom-call(f32[1,2,128,128]{3,2,1,0:T(8,128)} %onsite_in.1, f32[1,2,128,128]{3,2,1,0:T(8,128)} %hopping_in.1, f32[1,1,2,128,128]{4,3,2,1,0:T(8,128)} %sigma_in.1, f32[1,1,2,3,2,128,128]{6,5,4,3,2,1,0:T(8,128)} %screened.1), custom_call_target="tpu_custom_call" | custom-call | tf_op jit(solution)/shard_map/transport/pallas_call | solution.py:687
  67.2 0.7 %copy.8 = f32[1,1,3,2,128,128]{5,4,3,2,1,0:T(8,128)} copy(f32[1,1,3,2,128,128]{5,4,3,2,1,0:T(8,128)S(1)} %get-tuple-element.4) | data formatting | bytes 786432
  67.9 0.9 %copy.9 = f32[1,1,2,3,2,128,128]{6,5,4,3,2,1,0:T(8,128)} copy(f32[1,1,2,3,2,128,128]{6,5,4,3,2,1,0:T(8,128)S(1)} %get-tuple-element.5) | data formatting | bytes 1572864

commit v4 on v3

--- a/solution.py
+++ b/solution.py
@@ -208,9 +208,9 @@
     raw, c1, c1h, c2, c2h, c3, c3h, c4, c4h,
     m, x, r, y, v, t, k, kp, w1, w1p, f, fp, base, pa, pb,
     b_g0, b_g1, b_g2, b_a3, b_mo, b_k, b_kp, b_r, b_z,
-    spectral, wbuf, dbuf, scaled, factor, sbuf,
-    s_in, s_mat, s_w, s_d, s_relay, s_sig,
-    r_raw, r_mat, r_w, r_d, r_relay, r_sig,
+    spectral, wbuf, packed, dbuf, scaled, factor, sbuf,
+    s_in, s_mat, s_w, s_d, s_sig,
+    r_raw, r_mat, r_w, r_d, r_sig,
 ):
     e = lax.axis_index("energy")
     j = lax.axis_index("space")
@@ -220,7 +220,6 @@
     right = jnp.logical_not(left)
     place = jnp.where(left, j, NC - 1 - j)
     own = jnp.where(left, j, NC - j)
-    row = pl.multiple_of(chip * 8, 8)
 
     def at(p):
         return jnp.where(left, p, NC - 1 - p)
@@ -236,7 +235,7 @@
     for load in loads:
         load.start()
     own_w = pltpu.make_async_copy(
-        screened.at[0, 0, core, :, :, pl.ds(row, 8), :], wbuf.at[e], s_in.at[3]
+        screened.at[0, 0, :, :, :, e], wbuf.at[e], s_in.at[3]
     )
     own_w.start()
     barrier = pltpu.get_barrier_semaphore()
@@ -340,11 +339,9 @@
     send(place == 2, x, b_g2, 2, at(3))
 
     def send_w(i, c):
-        other = relative(i // 2)
-        kind = (core + i % 2) % 2
+        other = relative(i // 2) * 2 + (core + i % 2) % 2
         to_energy(
-            screened.at[0, 0, kind, :, :, pl.ds(pl.multiple_of(other * 8, 8), 8), :],
-            wbuf.at[e], s_w, r_w, other * 2 + kind,
+            screened.at[0, 0, :, :, :, other], wbuf.at[e], s_w, r_w, other
         ).start()
         return c
 
@@ -352,7 +349,7 @@
 
     def occupations(n, c):
         f = 1.0 / (1.0 + jnp.exp(energy_of(n, (8, B)) / THERMAL))
-        factor[n] = jnp.where(jnp.full((8, B), core, jnp.int32) == 0, -f, 1.0 - f)
+        factor[n] = jnp.where(lax.broadcasted_iota(jnp.int32, (8, B), 0) < 4, -f, 1.0 - f)
         return c
 
     @pl.when(place != 1)
@@ -586,55 +583,62 @@
         put(g, plus(b_r, mm(w, pb)))
         put(u, mm(b_z, pb))
 
-    spectral[0, 0] = g[0] - g[0].T
-    spectral[0, 1] = g[1] + g[1].T
     dr = u[0] - w[0].T
     di = u[1] + w[1].T
-    spectral[1, 0] = dr
-    spectral[1, 1] = di
-    spectral[2, 0] = -dr.T
-    spectral[2, 1] = di.T
-
-    near = sorted(range(1, NE // 2), key=lambda i: min(i // 4, 4 - i // 4) + min(i % 4, 4 - i % 4))
-    for i in near[::-1]:
-        other = relative(i)
-        to_energy(
-            spectral.at[:, :, pl.ds(pl.multiple_of(other * 8, 8), 8), :],
-            dbuf.at[core, chip], s_d, r_d.at[i], other * 2 + core,
-        ).start()
-    dbuf[core, chip] = spectral[:, :, pl.ds(row, 8), :]
-    sibling = chip * 2 + 1 - core
-
-    def pass_on(source):
-        piece = dbuf.at[core, source]
-        to_energy(piece, piece, s_relay, r_relay, sibling).start()
-
-    for i in near:
-        source = ((cx + 4 - i // 4) % 4) * 4 + (cy + 4 - i % 4) % 4
-        piece = dbuf.at[core, source]
-        to_energy(piece, piece, s_d, r_d.at[i], e).wait_recv()
-        pass_on(source)
-    pass_on(chip)
-    some = dbuf.at[0, pl.ds(0, NE // 2 - 1)]
-    relay = to_energy(dbuf.at[0], dbuf.at[0], s_relay, r_relay, sibling)
+    parts = (
+        (g[0] - g[0].T, g[1] + g[1].T),
+        (dr, di),
+        (-dr.T, di.T),
+    )
+    for b in range(3):
+        for c in range(2):
+            for i in range(NE):
+                spectral[b, c, i] = parts[b][c][4 * i : 4 * i + 4, :]
+
+    def hops(i):
+        return min(i // 4, 4 - i // 4) + min(i % 4, 4 - i % 4)
+
+    for i in sorted(range(NE // 2), key=hops, reverse=True):
+        for other_core in (1 - core, core):
+            if i == 0 and other_core is core:
+                continue
+            other = relative(i) * 2 + other_core
+            to_energy(spectral.at[:, :, other], dbuf.at[e], s_d, r_d, other).start()
+
+    dbuf[e] = spectral[:, :, e]
+    some = dbuf.at[pl.ds(0, NE - 1)]
     many = wbuf.at[pl.ds(0, NE - 1)]
     own_w.wait()
     to_energy(many, many, s_w, r_w, e).wait_recv()
-    relay.wait_recv()
+
+    def pack(n, c):
+        for b in range(3):
+            for i in range(2):
+                packed[n, b, i] = jnp.concatenate([wbuf[n, 0, b, i], wbuf[n, 1, b, i]])
+        return c
+
+    lax.fori_loop(0, NE, pack, 0)
+    to_energy(some, some, s_d, r_d, e).wait_recv()
 
     def scale(n, c):
-        scaled[8 + n] = dbuf[n % 2, n // 2] * factor[n]
+        for b in range(3):
+            for i in range(2):
+                one = dbuf[n, b, i]
+                scaled[8 + n, b, i] = jnp.concatenate([one, one]) * factor[n]
         return c
 
     lax.fori_loop(0, NE, scale, 0)
 
+    def far(i):
+        return jnp.where(i == 0, 2, jnp.where(i == 3, 0, 2 * i - 1))
+
     def convolve(turn, c):
-        start = ((cx + turn) % 4) * 8
+        start = ((cx + far(turn)) % 4) * 8
         for b in range(3):
             zero = jnp.zeros((8, B), F32)
 
             def add(k, acc):
-                wr, wi = wbuf[k, b, 0], wbuf[k, b, 1]
+                wr, wi = packed[k, b, 0], packed[k, b, 1]
                 new = []
                 for i in range(8):
                     lr = scaled[8 + start + i - k, b, 0]
@@ -650,16 +654,18 @@
 
             acc = lax.fori_loop(0, start // 8 + 1, add8, tuple((zero, zero) for _ in range(8)))
             for i in range(8):
-                sbuf[start + i, b, 0] = -acc[i][1]
-                sbuf[start + i, b, 1] = acc[i][0]
+                for kind in range(2):
+                    part = slice(4 * kind, 4 * kind + 4)
+                    sbuf[start + i, kind, b, 0] = -acc[i][1][part]
+                    sbuf[start + i, kind, b, 1] = acc[i][0][part]
 
         def send_s(i, c2):
-            n = start + (i + 2 * cy) % 8
+            n = start + ((cy + far(i // 2)) % 4) * 2 + (core + 1 + i) % 2
 
             @pl.when(n != e)
             def _():
                 to_energy(
-                    sbuf.at[n], out.at[0, 0, core, :, :, pl.ds(row, 8), :], s_sig, r_sig, n
+                    sbuf.at[n], out.at[0, 0, :, :, :, e], s_sig, r_sig, n
                 ).start()
 
             return c2
@@ -668,14 +674,13 @@
         return c
 
     lax.fori_loop(0, 4, convolve, 0)
-    out[0, 0, core, :, :, pl.ds(row, 8), :] = sbuf[e]
+    out[0, 0, :, :, :, e] = sbuf[e]
 
     for cond, copy in pending:
         pl.when(cond)(copy.wait_send)
 
     to_energy(many, many, s_w, r_w, e).wait_send()
-    to_energy(some, some, s_d, r_d.at[0], e).wait_send()
-    relay.wait_send()
+    to_energy(some, some, s_d, r_d, e).wait_send()
     to_energy(many, many, s_sig, r_sig, e).wait_send()
     to_energy(many, many, s_sig, r_sig, e).wait_recv()
 
@@ -684,11 +689,12 @@
     vmem = pl.BlockSpec(memory_space=pltpu.VMEM)
     hbm = pl.BlockSpec(memory_space=pltpu.HBM)
     square = pltpu.VMEM((2, B, B), F32)
-    return pl.pallas_call(
+    screened = screened.reshape(1, 1, 2, 3, 2, NE, 4, B)
+    green, out = pl.pallas_call(
         kernel,
         out_shape=(
             jax.ShapeDtypeStruct((1, 1, 3, 2, B, B), F32),
-            jax.ShapeDtypeStruct((1, 1, 2, 3, 2, B, B), F32),
+            jax.ShapeDtypeStruct((1, 1, 2, 3, 2, NE, 4, B), F32),
         ),
         in_specs=[hbm] * 4,
         out_specs=(vmem, vmem),
@@ -696,23 +702,24 @@
         + [pltpu.VMEM((5, 2, B, B), F32)]
         + [square] * 32
         + [
-            pltpu.VMEM((3, 2, B, B), F32),
+            pltpu.VMEM((3, 2, NE, 4, B), F32),
+            pltpu.VMEM((NE, 2, 3, 2, 4, B), F32),
             pltpu.VMEM((NE, 3, 2, 8, B), F32),
-            pltpu.VMEM((2, NE // 2, 3, 2, 8, B), F32),
+            pltpu.VMEM((NE, 3, 2, 4, B), F32),
             pltpu.VMEM((NE + 8, 3, 2, 8, B), F32),
             pltpu.VMEM((NE, 8, B), F32),
-            pltpu.VMEM((NE, 3, 2, 8, B), F32),
+            pltpu.VMEM((NE, 2, 3, 2, 4, B), F32),
         ]
         + [pltpu.SemaphoreType.DMA((4,)), pltpu.SemaphoreType.DMA((32,))]
-        + [pltpu.SemaphoreType.DMA] * 4
+        + [pltpu.SemaphoreType.DMA] * 3
         + [pltpu.SemaphoreType.DMA((5,)), pltpu.SemaphoreType.DMA((9,))]
-        + [pltpu.SemaphoreType.DMA, pltpu.SemaphoreType.DMA((NE // 2,))]
-        + [pltpu.SemaphoreType.DMA] * 2,
+        + [pltpu.SemaphoreType.DMA] * 3,
         compiler_params=pltpu.CompilerParams(
             collective_id=0, has_side_effects=True, vmem_limit_bytes=48 * 2**20
         ),
         name="transport",
     )(*(pltpu.with_memory_space_constraint(a, pltpu.HBM) for a in (onsite, hopping, sigma_old, screened)))
+    return green, out.reshape(1, 1, 2, 3, 2, B, B)
 
 
 def solution(mesh):

time: 68.9 us -> 66.1 us (0.959)
  Pallas kernels: 66.6 us -> 63.8 us
    pallas_call x1, Pallas kernels: 66.6 us -> 63.8 us  [local(): pl.pallas_call(kernel, out_shape=(jax.ShapeDtypeStruct((1, 1, 3, 2, B, B)...]
where the time goes in v4:
time: 66.1 us; the launch traced here: 66 us
  Pallas kernels  63.8 us (97%)
  local copies, waits for them, and re-layouts  1.63 us (2%)
    pallas_call x1, Pallas kernels, local(): pl.pallas_call(kernel, out_shape=(jax.ShapeDtypeStruct((1, 1, 3, 2, B, B)...  63.8 us
    unnamed x2, local copies, waits for them, and re-layouts  1.63 us

profile of v4, /device:TPU:1, one launch (start us, length us, event | category | flops | bytes accessed | tf_op | source)
XLA Modules:
  0.0 66.0 jit_solution(6957909777759634744)
XLA Ops:
  0.6 63.8 %transport.1 = (f32[1,1,3,2,128,128]{5,4,3,2,1,0:T(8,128)S(1)}, f32[1,1,2,3,2,32,4,128]{7,6,5,4,3,2,1,0:T(4,128)S(1)}) custom-call(f32[1,2,128,128]{3,2,1,0:T(8,128)} %onsite_in.1, f32[1,2,128,128]{3,2,1,0:T(8,128)} %hopping_in.1, f32[1,1,2,128,128]{4,3,2,1,0:T(8,128)} %sigma_in.1, f32[1,1,2,3,2,32,4,128]{7,6,5,4,3,2,1,0:T(4,128)} %bitcast.3), custom_call_target="tpu_custom_call" | custom-call | tf_op jit(solution)/shard_map/transport/pallas_call | solution.py:693
  64.4 0.7 %copy.8 = f32[1,1,3,2,128,128]{5,4,3,2,1,0:T(8,128)} copy(f32[1,1,3,2,128,128]{5,4,3,2,1,0:T(8,128)S(1)} %get-tuple-element.8) | data formatting | bytes 786432
  65.1 0.9 %copy.9 = f32[1,1,2,3,2,128,128]{6,5,4,3,2,1,0:T(8,128)} copy(f32[1,1,2,3,2,128,128]{6,5,4,3,2,1,0:T(8,128)S(1)} %bitcast.2) | data formatting | bytes 1572864

commit v5 on v4

--- a/solution.py
+++ b/solution.py
@@ -443,9 +443,9 @@
         put(pb, mm(pa, y))
         put(b_z, plus(r, mm(pb, base)))
 
+    send(place == 1, b_z, b_z, 8, at(0))
     send(place == 1, b_z, b_z, 8, at(2))
     send(left & (place == 1), b_z, b_z, 8, 3)
-    send(place == 1, b_z, b_z, 8, at(0))
 
     @pl.when(place == 1)
     def _():
@@ -615,6 +615,7 @@
         for b in range(3):
             for i in range(2):
                 packed[n, b, i] = jnp.concatenate([wbuf[n, 0, b, i], wbuf[n, 1, b, i]])
+            packed[n, b, 2] = packed[n, b, 0] + packed[n, b, 1]
         return c
 
     lax.fori_loop(0, NE, pack, 0)
@@ -625,6 +626,7 @@
             for i in range(2):
                 one = dbuf[n, b, i]
                 scaled[8 + n, b, i] = jnp.concatenate([one, one]) * factor[n]
+            scaled[8 + n, b, 2] = scaled[8 + n, b, 0] + scaled[8 + n, b, 1]
         return c
 
     lax.fori_loop(0, NE, scale, 0)
@@ -638,13 +640,14 @@
             zero = jnp.zeros((8, B), F32)
 
             def add(k, acc):
-                wr, wi = packed[k, b, 0], packed[k, b, 1]
+                wr, wi, ws = packed[k, b, 0], packed[k, b, 1], packed[k, b, 2]
                 new = []
                 for i in range(8):
                     lr = scaled[8 + start + i - k, b, 0]
                     li = scaled[8 + start + i - k, b, 1]
-                    ar, ai = acc[i]
-                    new.append((ar + (lr * wr - li * wi), ai + (lr * wi + li * wr)))
+                    ls = scaled[8 + start + i - k, b, 2]
+                    rr, ii, both = acc[i]
+                    new.append((rr + lr * wr, ii + li * wi, both + ls * ws))
                 return tuple(new)
 
             def add8(k, acc):
@@ -652,12 +655,13 @@
                     acc = add(k * 8 + s, acc)
                 return acc
 
-            acc = lax.fori_loop(0, start // 8 + 1, add8, tuple((zero, zero) for _ in range(8)))
+            acc = lax.fori_loop(0, start // 8 + 1, add8, tuple((zero, zero, zero) for _ in range(8)))
             for i in range(8):
+                rr, ii, both = acc[i]
                 for kind in range(2):
                     part = slice(4 * kind, 4 * kind + 4)
-                    sbuf[start + i, kind, b, 0] = -acc[i][1][part]
-                    sbuf[start + i, kind, b, 1] = acc[i][0][part]
+                    sbuf[start + i, kind, b, 0] = (rr + ii - both)[part]
+                    sbuf[start + i, kind, b, 1] = (rr - ii)[part]
 
         def send_s(i, c2):
             n = start + ((cy + far(i // 2)) % 4) * 2 + (core + 1 + i) % 2
@@ -704,9 +708,9 @@
         + [
             pltpu.VMEM((3, 2, NE, 4, B), F32),
             pltpu.VMEM((NE, 2, 3, 2, 4, B), F32),
-            pltpu.VMEM((NE, 3, 2, 8, B), F32),
+            pltpu.VMEM((NE, 3, 3, 8, B), F32),
             pltpu.VMEM((NE, 3, 2, 4, B), F32),
-            pltpu.VMEM((NE + 8, 3, 2, 8, B), F32),
+            pltpu.VMEM((NE + 8, 3, 3, 8, B), F32),
             pltpu.VMEM((NE, 8, B), F32),
             pltpu.VMEM((NE, 2, 3, 2, 4, B), F32),
         ]

time: 66.1 us -> 66.1 us (level)
  no operation moved by 1% of the time
where the time goes in v5:
time: 66.1 us; the launch traced here: 66 us
  Pallas kernels  63.7 us (96%)
  local copies, waits for them, and re-layouts  1.63 us (2%)
    pallas_call x1, Pallas kernels, local(): pl.pallas_call(kernel, out_shape=(jax.ShapeDtypeStruct((1, 1, 3, 2, B, B)...  63.7 us
    unnamed x2, local copies, waits for them, and re-layouts  1.63 us

profile of v5, /device:TPU:1, one launch (start us, length us, event | category | flops | bytes accessed | tf_op | source)
XLA Modules:
  0.0 66.0 jit_solution(8737275464077378687)
XLA Ops:
  0.6 63.7 %transport.1 = (f32[1,1,3,2,128,128]{5,4,3,2,1,0:T(8,128)S(1)}, f32[1,1,2,3,2,32,4,128]{7,6,5,4,3,2,1,0:T(4,128)S(1)}) custom-call(f32[1,2,128,128]{3,2,1,0:T(8,128)} %onsite_in.1, f32[1,2,128,128]{3,2,1,0:T(8,128)} %hopping_in.1, f32[1,1,2,128,128]{4,3,2,1,0:T(8,128)} %sigma_in.1, f32[1,1,2,3,2,32,4,128]{7,6,5,4,3,2,1,0:T(4,128)} %bitcast.3), custom_call_target="tpu_custom_call" | custom-call | tf_op jit(solution)/shard_map/transport/pallas_call | solution.py:697
  64.4 0.7 %copy.8 = f32[1,1,3,2,128,128]{5,4,3,2,1,0:T(8,128)} copy(f32[1,1,3,2,128,128]{5,4,3,2,1,0:T(8,128)S(1)} %get-tuple-element.8) | data formatting | bytes 786432
  65.1 0.9 %copy.9 = f32[1,1,2,3,2,128,128]{6,5,4,3,2,1,0:T(8,128)} copy(f32[1,1,2,3,2,128,128]{6,5,4,3,2,1,0:T(8,128)S(1)} %bitcast.2) | data formatting | bytes 1572864
